TPU v7x, 512 devices: a whole 4x4x16 slice. The times are simulated.
512 devices in a mesh: lon: 16 (over z), lat: 8 (over y, core), tp: 4 (over x).
Axes of the slice: x: 4, y: 4, z: 16, core: 2. Of those that a mesh axis runs over, the one named last changes fastest.
Arguments:
- features: bfloat16 [8, 2048, 2048], P('lat', 'lon', 'tp'), may hold values from -6 to 6
- projections: bfloat16 [8, 2048, 256], P('lat', 'lon'), may hold values from -6 to 6
- step_raw: float32 [8, 2048, 32], P('lat', 'lon', 'tp'), may hold values from -4 to 4
- step_bias: float32 [32], P('tp'), may hold values from -1 to 0.5
- decay_log: float32 [2, 32], P(None, 'tp'), may hold values from -8.5 to -2.3
- skip_gain: float32 [32], P('tp'), may hold values from 0.5 to 1.5
- conv_features: float32 [9, 2048], P(None, 'tp'), may hold values from -2 to 2
- conv_projections: float32 [9, 256], replicated, may hold values from -0.25 to 0.25
- state_east: float32 [8, 32, 64, 128], P('lat', 'tp'), may hold values from -6 to 6
- state_west: float32 [8, 32, 64, 128], P('lat', 'tp'), may hold values from -6 to 6
- cotangent: bfloat16 [8, 2048, 2048], P('lat', 'lon', 'tp'), may hold values from -6 to 6
Outputs:
- mixed: bfloat16 [8, 2048, 2048], P('lat', 'lon', 'tp')
- grad_features: bfloat16 [8, 2048, 2048], P('lat', 'lon', 'tp')
- grad_projections: bfloat16 [8, 2048, 256], P('lat', 'lon')
- grad_step: float32 [8, 2048, 32], P('lat', 'lon', 'tp')
- grad_conv_features: float32 [9, 2048], P(None, 'tp')
- grad_conv_projections: float32 [9, 256], replicated
- grad_decay_log: float32 [2, 32], P(None, 'tp')
- grad_step_bias: float32 [32], P('tp')
- grad_skip_gain: float32 [32], P('tp')
All inputs are finite; a program needn't handle non-finite values.
Results may differ from a plain program's by a relative error of at most 0.0065.
Values may be sent and summed in bfloat16 or wider, within the bound.
A program may use at most 128 MiB of HBM per device.

v0:
```python
from functools import partial

import jax
import jax.numpy as jnp
from jax import lax
from jax.sharding import PartitionSpec as P

PRECISE = lax.Precision.HIGHEST


def extended(block, sides, width):
    for axis, dim in sides:
        count = lax.axis_size(axis)
        forward = [(i, i + 1) for i in range(count - 1)]
        backward = [(target, source) for source, target in forward]
        low = lax.ppermute(
            lax.slice_in_dim(block, block.shape[dim] - width, None, axis=dim), axis, forward
        )
        high = lax.ppermute(lax.slice_in_dim(block, 0, width, axis=dim), axis, backward)
        block = jnp.concatenate([low, block, high], axis=dim)
    return block


def prefix(value, axis, join, neutral, backward):
    count, mine = (lax.axis_size(axis), lax.axis_index(axis))
    pieces = jax.tree.map(lambda part: lax.all_gather(part, axis), value)
    if backward:
        pieces = jax.tree.map(lambda part: part[::-1], pieces)
        mine = count - 1 - mine
    total = jax.tree.map(
        lambda part, zero: jnp.full_like(part, 0) + jnp.asarray(zero, part.dtype), value, neutral
    )

    def step(position, total):
        longer = join(total, jax.tree.map(lambda part: part[position], pieces))
        return jax.tree.map(lambda new, old: jnp.where(position < mine, new, old), longer, total)

    return lax.fori_loop(0, count - 1, step, total)


def log_decay(step_sizes, rates):
    return jnp.cumsum(-step_sizes * rates, axis=1)


def block_ends(inner, b_part, step_sizes, rates):
    decay_sum = log_decay(step_sizes, rates)
    closing = decay_sum[:, -1:, :]
    factor = jnp.exp(closing - decay_sum) * step_sizes
    scaled = factor[..., None] * inner
    summed = jnp.einsum("rjhp,rjn->rhpn", scaled, b_part, precision=PRECISE)
    return (jnp.exp(closing[:, 0, :]), summed)


def head_mix(inner_head, scores, decay_head, steps_head):
    count = scores.shape[1]
    causal = lax.broadcasted_iota(jnp.int32, (count, count), 0) >= lax.broadcasted_iota(
        jnp.int32, (count, count), 1
    )
    spread = jnp.where(causal, decay_head[:, :, None] - decay_head[:, None, :], 0.0)
    mixing = jnp.where(causal, jnp.exp(spread), 0.0) * scores * steps_head[:, None, :]
    return jnp.einsum("rij,rjp->rip", mixing, inner_head, precision=PRECISE)


def block_mix(inner, b_part, c_part, step_sizes, rates):
    decay_sum = log_decay(step_sizes, rates)
    scores = jnp.einsum("rin,rjn->rij", c_part, b_part, precision=PRECISE)
    mixer = jax.checkpoint(head_mix)
    results = [
        mixer(inner[:, :, member, :], scores, decay_sum[:, :, member], step_sizes[:, :, member])
        for member in range(inner.shape[2])
    ]
    return jnp.stack(results, axis=2)


def block_reads(c_part, step_sizes, rates, entering):
    decay_sum = log_decay(step_sizes, rates)
    reading = jnp.einsum("rin,rhpn->rihp", c_part, entering, precision=PRECISE)
    return reading * jnp.exp(decay_sum)[..., None]


def block_sources(c_part, step_sizes, rates, incoming):
    decay_sum = log_decay(step_sizes, rates)
    weighted = incoming * jnp.exp(decay_sum)[..., None]
    return jnp.einsum("rihp,rin->rhpn", weighted, c_part, precision=PRECISE)


def combine(earlier, later):
    return (earlier[0] * later[0], later[0][..., None, None] * earlier[1] + later[1])


def stencil(padded, kernel, row_count, col_count):
    total = jnp.zeros((row_count, col_count, padded.shape[2]), jnp.float32)
    for offset_row in range(3):
        for offset_col in range(3):
            total = total + kernel[3 * offset_row + offset_col] * padded[
                offset_row : offset_row + row_count, offset_col : offset_col + col_count
            ].astype(jnp.float32)
    return total


def stencil_adjoint(padded, kernel, row_count, col_count):
    total = jnp.zeros((row_count, col_count, padded.shape[2]), jnp.float32)
    for offset_row in range(3):
        for offset_col in range(3):
            total = total + kernel[3 * offset_row + offset_col] * padded[
                2 - offset_row : 2 - offset_row + row_count,
                2 - offset_col : 2 - offset_col + col_count,
            ].astype(jnp.float32)
    return total


def stencil_weights(grads, padded, row_count, col_count):
    grads32 = grads.astype(jnp.float32)
    rows_out = []
    for offset_row in range(3):
        for offset_col in range(3):
            window = padded[
                offset_row : offset_row + row_count, offset_col : offset_col + col_count
            ].astype(jnp.float32)
            rows_out.append(jnp.sum(grads32 * window, axis=(0, 1)))
    return jnp.stack(rows_out)


def shards(
    features,
    projections,
    step_raw,
    step_bias,
    decay_log,
    skip_gain,
    conv_features,
    conv_projections,
    state_east,
    state_west,
    cotangent,
):
    row_count, col_count, width = features.shape
    heads_here = step_raw.shape[2]
    head_size = width // heads_here
    state_size = projections.shape[2] // 2
    joined = jnp.concatenate([features, projections], axis=2)
    kernel = jnp.concatenate([conv_features, conv_projections], axis=1)
    padded = extended(joined, (("lat", 0), ("lon", 1)), 1)
    before = stencil(padded, kernel, row_count, col_count)
    active = jax.nn.silu(before).astype(jnp.bfloat16)
    inner = (
        active[:, :, :width]
        .astype(jnp.float32)
        .reshape(row_count, col_count, heads_here, head_size)
    )
    b_part = active[:, :, width : width + state_size].astype(jnp.float32)
    c_part = active[:, :, width + state_size :].astype(jnp.float32)
    shifted = step_raw + step_bias
    step_sizes = jax.nn.softplus(shifted)
    rates = jnp.exp(decay_log)
    incoming = cotangent.reshape(row_count, col_count, heads_here, head_size).astype(jnp.float32)
    inner_back = jnp.flip(inner, 1)
    b_back = jnp.flip(b_part, 1)
    c_back = jnp.flip(c_part, 1)
    steps_back = jnp.flip(step_sizes, 1)
    incoming_back = jnp.flip(incoming, 1)
    ends_east, pull_ends_east = jax.vjp(block_ends, inner, b_part, step_sizes, rates[0])
    ends_west, pull_ends_west = jax.vjp(block_ends, inner_back, b_back, steps_back, rates[1])
    neutral = (
        jnp.ones((row_count, heads_here), jnp.float32),
        jnp.zeros((row_count, heads_here, head_size, state_size), jnp.float32),
    )
    prefix_east = prefix(ends_east, "lon", combine, neutral, False)
    prefix_west = prefix(ends_west, "lon", combine, neutral, True)
    entering_east = prefix_east[0][..., None, None] * state_east + prefix_east[1]
    entering_west = prefix_west[0][..., None, None] * state_west + prefix_west[1]
    mix_east, pull_mix_east = jax.vjp(block_mix, inner, b_part, c_part, step_sizes, rates[0])
    mix_west, pull_mix_west = jax.vjp(block_mix, inner_back, b_back, c_back, steps_back, rates[1])
    read_east, pull_read_east = jax.vjp(
        partial(block_reads, entering=entering_east), c_part, step_sizes, rates[0]
    )
    read_west, pull_read_west = jax.vjp(
        partial(block_reads, entering=entering_west), c_back, steps_back, rates[1]
    )
    mixed32 = mix_east + read_east + jnp.flip(mix_west + read_west, 1) + skip_gain[:, None] * inner
    mixed = mixed32.reshape(row_count, col_count, width).astype(jnp.bfloat16)
    source_east = block_sources(c_part, step_sizes, rates[0], incoming)
    source_west = block_sources(c_back, steps_back, rates[1], incoming_back)
    adjoint_east = prefix((ends_east[0], source_east), "lon", combine, neutral, True)[1]
    adjoint_west = prefix((ends_west[0], source_west), "lon", combine, neutral, False)[1]
    grad_mix_east = pull_mix_east(incoming)
    grad_mix_west = pull_mix_west(incoming_back)
    grad_read_east = pull_read_east(incoming)
    grad_read_west = pull_read_west(incoming_back)
    grad_ends_east = pull_ends_east(
        (jnp.sum(adjoint_east * entering_east, axis=(2, 3)), adjoint_east)
    )
    grad_ends_west = pull_ends_west(
        (jnp.sum(adjoint_west * entering_west, axis=(2, 3)), adjoint_west)
    )
    grad_inner = (
        grad_mix_east[0]
        + grad_ends_east[0]
        + jnp.flip(grad_mix_west[0] + grad_ends_west[0], 1)
        + skip_gain[:, None] * incoming
    )
    grad_b = (
        grad_mix_east[1] + grad_ends_east[1] + jnp.flip(grad_mix_west[1] + grad_ends_west[1], 1)
    )
    grad_c = (
        grad_mix_east[2] + grad_read_east[0] + jnp.flip(grad_mix_west[2] + grad_read_west[0], 1)
    )
    grad_steps = (
        grad_mix_east[3]
        + grad_read_east[1]
        + grad_ends_east[2]
        + jnp.flip(grad_mix_west[3] + grad_read_west[1] + grad_ends_west[2], 1)
    )
    grad_rates = jnp.stack(
        [
            grad_mix_east[4] + grad_read_east[2] + grad_ends_east[3],
            grad_mix_west[4] + grad_read_west[2] + grad_ends_west[3],
        ]
    )
    grad_gain = jnp.sum(incoming * inner, axis=(0, 1, 3))
    grad_proj = lax.psum(jnp.concatenate([grad_b, grad_c], axis=2), "tp").astype(jnp.bfloat16)
    grad_active = jnp.concatenate(
        [grad_inner.reshape(row_count, col_count, width).astype(jnp.bfloat16), grad_proj], axis=2
    )
    slope = jax.nn.sigmoid(before)
    grad_before = (grad_active.astype(jnp.float32) * slope * (1.0 + before * (1.0 - slope))).astype(
        jnp.bfloat16
    )
    grad_padded = extended(grad_before, (("lat", 0), ("lon", 1)), 1)
    grad_joined = stencil_adjoint(grad_padded, kernel, row_count, col_count)
    grad_kernel = stencil_weights(grad_before, padded, row_count, col_count)
    grad_raw = grad_steps * jax.nn.sigmoid(shifted)
    totals = lax.psum(
        (grad_kernel, grad_rates * rates, jnp.sum(grad_raw, axis=(0, 1)), grad_gain), ("lon", "lat")
    )
    scale = (row_count * lax.axis_size("lat") * col_count * lax.axis_size("lon")) ** (-0.5)
    return (
        mixed,
        grad_joined[:, :, :width].astype(jnp.bfloat16),
        grad_joined[:, :, width:].astype(jnp.bfloat16),
        grad_raw,
        totals[0][:, :width] * scale,
        totals[0][:, width:] * scale,
        totals[1] * scale,
        totals[2] * scale,
        totals[3] * scale,
    )


def solution(mesh):
    in_specs = (
        P("lat", "lon", "tp"),
        P("lat", "lon", None),
        P("lat", "lon", "tp"),
        P("tp"),
        P(None, "tp"),
        P("tp"),
        P(None, "tp"),
        P(),
        P("lat", "tp", None, None),
        P("lat", "tp", None, None),
        P("lat", "lon", "tp"),
    )
    out_specs = (
        P("lat", "lon", "tp"),
        P("lat", "lon", "tp"),
        P("lat", "lon", None),
        P("lat", "lon", "tp"),
        P(None, "tp"),
        P(),
        P(None, "tp"),
        P("tp"),
        P("tp"),
    )
    return jax.shard_map(shards, mesh=mesh, in_specs=in_specs, out_specs=out_specs, check_vma=False)
```

profile of v0, /device:TPU:1, one launch (start us, length us, event | category | flops | bytes accessed | tf_op | source)
XLA Modules:
  0.0 948.4 jit_solution(10290589166438115905)
XLA Ops:
  9.0 8.7 collective-permute-start.1
  17.8 1.9 collective-permute-start
  27.0 2.4 collective-permute-done.3
  32.1 26.6 %all_gather.36 = f32[16,1,8]{2,1,0:T(1,128)S(1)} all-gather(f32[1,1,8]{2,1,0:T(1,128)S(1)} %get-tuple-element.971), channel_id=1, replica_groups=mesh['lon'=16,'lat'=8,'tp'=4] {'lon'}, dimensions={0}, use_global_device_ids=true | all-gather | bytes 544 | tf_op jit(solution)/shard_map/all_gather | solution.py:26
  59.5 21.7 %all_gather.39 = f32[16,1,8]{2,1,0:T(1,128)S(1)} all-gather(f32[1,1,8]{2,1,0:T(1,128)S(1)} %get-tuple-element.983), channel_id=1, replica_groups=mesh['lon'=16,'lat'=8,'tp'=4] {'lon'}, dimensions={0}, use_global_device_ids=true | all-gather | bytes 544 | tf_op jit(solution)/shard_map/all_gather | solution.py:26
  103.6 1.4 slice.401
  107.9 1.4 slice.389
  109.4 1.4 slice.385
  112.2 1.4 slice.377
  113.7 2.4 fusion.146
  117.4 2.3 fusion.140
  121.1 2.3 fusion.141
  124.8 2.3 fusion.142
  128.5 2.3 fusion.143
  132.2 2.3 fusion.144
  137.9 1.7 fusion.145
  139.6 2.1 multiply_add_fusion.5
  141.7 1.5 fusion.139
  147.2 2.6 reduce_window_sum.67
  152.5 2.3 fusion.109
  156.2 2.3 fusion.108
  159.9 2.3 fusion.107
  163.6 2.3 fusion.106
  167.3 2.3 fusion.105
  171.0 2.3 fusion.104
  179.0 1.7 fusion.103
  180.7 2.1 multiply_add_fusion.4
  182.8 1.5 fusion.102
  186.6 2.6 reduce_window_sum.70
  192.1 1.7 convolution_bitcast_fusion.3
  193.8 1.7 convolution_bitcast_fusion.2
  195.6 1.7 convolution_bitcast_fusion.8
  197.3 1.7 convolution_bitcast_fusion.9
  199.0 1.7 convolution_bitcast_fusion.10
  200.7 1.7 convolution_bitcast_fusion.11
  202.4 1.7 convolution_bitcast_fusion.12
  204.1 1.7 convolution_bitcast_fusion.13
  205.8 1.7 convolution_bitcast_fusion.14
  207.6 1.7 convolution_bitcast_fusion.15
  209.3 1.7 convolution_bitcast_fusion.22
  211.0 1.7 convolution_bitcast_fusion.21
  212.7 1.7 convolution_bitcast_fusion.20
  214.4 1.7 convolution_bitcast_fusion.19
  216.1 1.7 convolution_bitcast_fusion.18
  217.8 1.7 convolution_bitcast_fusion.17
  219.5 1.7 convolution_bitcast_fusion.16
  221.2 1.7 convolution_bitcast_fusion.23
  240.7 34.2 %while.60 = (s32[]{:T(128)}, f32[1,8]{1,0:T(1,128)}, f32[1,8,64,128]{3,2,1,0:T(8,128)S(1)}, s32[]{:T(128)}, f32[16,1,8]{2,1,0:T(1,128)S(1)}, /*index=5*/f32[16,1,8,64,128]{4,3,2,1,0:T(8,128)}, s32[]{:T(128)}, s32[]{:T(128)}) while((s32[]{:T(128)}, f32[1,8]{1,0:T(1,128)}, f32[1,8,64,128]{3,2,1,0:T(8,128)S(1)}, s32[]{:T(128)}, ...), condition=%wide.region_2.3_spmd.clone, body=%wide.region_1.2_spmd.clone.sunk | while | flops 262172 | bytes 786751 | solution.py:38
  275.0 4.7 rev.48
  279.7 25.8 %while.62 = (s32[]{:T(128)}, f32[1,8,64,128]{3,2,1,0:T(8,128)S(1)}, s32[]{:T(128)}, f32[16,1,8]{2,1,0:T(1,128)}, f32[16,1,8,64,128]{4,3,2,1,0:T(8,128)}, /*index=5*/s32[]{:T(128)}, s32[]{:T(128)}) while((s32[]{:T(128)}, f32[1,8,64,128]{3,2,1,0:T(8,128)S(1)}, s32[]{:T(128)}, f32[16,1,8]{2,1,0:T(1,128)}, ...), condition=%wide.region_7.8_spmd.clone, body=%wide.region_6.7_spmd.clone.sunk | while | flops 262148 | bytes 786641 | solution.py:38
  305.4 1.7 multiply_reduce_fusion.3
  309.0 25.6 %while.63 = (s32[]{:T(128)}, f32[1,8,64,128]{3,2,1,0:T(8,128)S(1)}, s32[]{:T(128)}, f32[16,1,8]{2,1,0:T(1,128)}, f32[16,1,8,64,128]{4,3,2,1,0:T(8,128)}, /*index=5*/s32[]{:T(128)}, s32[]{:T(128)}) while((s32[]{:T(128)}, f32[1,8,64,128]{3,2,1,0:T(8,128)S(1)}, s32[]{:T(128)}, f32[16,1,8]{2,1,0:T(1,128)}, ...), condition=%wide.region_9.10_spmd.clone, body=%wide.region_8.9_spmd.clone.sunk | while | flops 262148 | bytes 786641 | solution.py:38
  334.7 4.7 rev.46
  339.4 35.4 %while.61 = (s32[]{:T(128)}, f32[1,8]{1,0:T(1,128)S(1)}, f32[1,8,64,128]{3,2,1,0:T(8,128)S(1)}, s32[]{:T(128)}, f32[16,1,8]{2,1,0:T(1,128)}, /*index=5*/f32[16,1,8,64,128]{4,3,2,1,0:T(8,128)}, s32[]{:T(128)}, s32[]{:T(128)}) while((s32[]{:T(128)}, f32[1,8]{1,0:T(1,128)S(1)}, f32[1,8,64,128]{3,2,1,0:T(8,128)S(1)}, s32[]{:T(128)}, ...), condition=%wide.region_5.6_spmd.clone, body=%wide.region_4.5_spmd.clone.sunk | while | flops 262172 | bytes 786751 | solution.py:38
  375.4 1.7 multiply_reduce_fusion.1
  378.7 1.4 fusion.8
  382.7 14.8 %all-reduce.52 = bf16[1,128,256]{2,1,0:T(8,128)(2,1)S(1)} all-reduce(f32[1,128,256]{2,1,0:T(8,128)S(1)} %pad_maximum_fusion.16), channel_id=1, replica_groups=mesh['lon'=16,'lat'=8,'tp'=4] {'tp'}, use_global_device_ids=true, to_apply=%region_10.11 | all-reduce | flops 32768 | bytes 196608 | tf_op jit(solution)/shard_map/psum | solution.py:221
  397.5 2.6 multiply_reduce_fusion.2
  401.1 1.8 multiply_reduce_fusion.4
  403.1 1.5 fusion.49
  404.6 17.3 %collective-permute-start.5 = (bf16[1,128,768]{2,1,0:T(8,128)(2,1)S(1)}, bf16[1,128,768]{2,1,0:T(8,128)(2,1)S(1)}, u32[]{:S(2)}, u32[]{:S(2)}) collective-permute-start(bf16[1,128,768]{2,1,0:T(8,128)(2,1)S(1)} %get-tuple-element.871), channel_id=1, source_target_pairs={{4,0},{8,4},{12,8},{16,12},{20,16},{24,20},{28,24},{5,1},{9,5},{13... | collective-permute-start | bytes 589832 | tf_op jit(solution)/shard_map/ppermute | solution.py:19
  421.9 3.6 collective-permute-start.4
  441.2 489.3 %all-reduce.50 = (f32[9,768]{1,0:T(8,128)S(1)}, f32[2,8]{1,0:T(2,128)S(1)}, f32[8]{0:T(128)S(1)}, f32[8]{0:T(128)S(1)}) all-reduce(f32[9,768]{1,0:T(8,128)S(1)} %stack.116, f32[2,8]{1,0:T(2,128)S(1)} %maximum_multiply_fusion, f32[8]{0:T(128)S(1)} %get-tuple-element.869, ...), channel_id=1, replica_groups=mesh['lon'=16,'lat'=8,'tp'=4] {'lon','lat'}, use_global_device_ids=true, to_apply=%region_82.83 | all-reduce | flops 6944 | bytes 55552 | tf_op jit(solution)/shard_map/psum | solution.py:233
  934.1 4.0 collective-permute-start.7
  (517 shorter events, 240.8 us)
Async XLA Ops:
  7.2 233.5 %all-gather.9.cloned.1.call-start = ((), (), s32[]{:S(2)}) async-start(), calls=%async_computation | async-start | bytes 4456448 | tf_op jit(solution)/shard_map/all_gather | solution.py:26
  9.0 14.6 %collective-permute-start.1 = (bf16[1,128,768]{2,1,0:T(8,128)(2,1)S(1)}, bf16[1,128,768]{2,1,0:T(8,128)(2,1)S(1)}, u32[]{:S(2)}, u32[]{:S(2)}) collective-permute-start(bf16[1,128,768]{2,1,0:T(8,128)(2,1)S(1)} %constant_dynamic-update-slice_fusion.2), channel_id=1, source_target_pairs={{4,0},{8,4},{12,8},{16,12},{20,16},{24,20},{28,24},{5,1},{9,5},{13... | collective-permute-start | bytes 589832 | tf_op jit(solution)/shard_map/ppermute | solution.py:19
  17.8 5.9 collective-permute-start
  20.4 39.1 %copy-start.47 = (f32[8]{0:T(128)}, f32[8]{0:T(128)S(1)}, u32[]{:S(2)}) copy-start(f32[8]{0:T(128)S(1)} %get-tuple-element.984) | copy-start | bytes 100
  23.7 3.2 collective-permute-start.2
  25.0 4.4 collective-permute-start.3
  26.4 55.6 %copy-start.12 = (f32[768]{0:T(1024)}, f32[768]{0:T(1024)S(1)}, u32[]{:S(2)}) copy-start(f32[768]{0:T(1024)S(1)} %get-tuple-element.812) | copy-start | bytes 9220
  26.4 55.6 %copy-start.14 = (f32[768]{0:T(1024)}, f32[768]{0:T(1024)S(1)}, u32[]{:S(2)}) copy-start(f32[768]{0:T(1024)S(1)} %get-tuple-element.813) | copy-start | bytes 9220
  26.4 55.6 %copy-start.16 = (f32[768]{0:T(1024)}, f32[768]{0:T(1024)S(1)}, u32[]{:S(2)}) copy-start(f32[768]{0:T(1024)S(1)} %get-tuple-element.814) | copy-start | bytes 9220
  26.4 55.6 %copy-start.18 = (f32[768]{0:T(1024)}, f32[768]{0:T(1024)S(1)}, u32[]{:S(2)}) copy-start(f32[768]{0:T(1024)S(1)} %get-tuple-element.815) | copy-start | bytes 9220
  26.4 55.6 %copy-start.20 = (f32[768]{0:T(1024)}, f32[768]{0:T(1024)S(1)}, u32[]{:S(2)}) copy-start(f32[768]{0:T(1024)S(1)} %get-tuple-element.816) | copy-start | bytes 9220
  26.4 55.6 %copy-start.22 = (f32[768]{0:T(1024)}, f32[768]{0:T(1024)S(1)}, u32[]{:S(2)}) copy-start(f32[768]{0:T(1024)S(1)} %get-tuple-element.817) | copy-start | bytes 9220
  26.4 55.6 %copy-start.24 = (f32[768]{0:T(1024)}, f32[768]{0:T(1024)S(1)}, u32[]{:S(2)}) copy-start(f32[768]{0:T(1024)S(1)} %get-tuple-element.818) | copy-start | bytes 9220
  26.5 55.6 %copy-start.26 = (f32[768]{0:T(1024)}, f32[768]{0:T(1024)S(1)}, u32[]{:S(2)}) copy-start(f32[768]{0:T(1024)S(1)} %get-tuple-element.819) | copy-start | bytes 9220
  26.5 55.6 %copy-start.28 = (f32[768]{0:T(1024)}, f32[768]{0:T(1024)S(1)}, u32[]{:S(2)}) copy-start(f32[768]{0:T(1024)S(1)} %get-tuple-element.820) | copy-start | bytes 9220
  27.0 55.1 %copy-start.33 = (bf16[3,1,768]{2,1,0:T(2,128)(2,1)}, bf16[3,1,768]{2,1,0:T(2,128)(2,1)S(1)}, u32[]{:S(2)}) copy-start(bf16[3,1,768]{2,1,0:T(2,128)(2,1)S(1)} %collective-permute-done.2) | copy-start | bytes 13828
  29.4 52.7 %copy-start.10 = (bf16[3,1,768]{2,1,0:T(2,128)(2,1)}, bf16[3,1,768]{2,1,0:T(2,128)(2,1)S(1)}, u32[]{:S(2)}) copy-start(bf16[3,1,768]{2,1,0:T(2,128)(2,1)S(1)} %collective-permute-done.3) | copy-start | bytes 13828
  31.9 243.1 %all-gather.13.cloned.1.call-start = ((), (), s32[]{:S(2)}) async-start(), calls=%async_computation.2 | async-start | bytes 4456448 | tf_op jit(solution)/shard_map/all_gather | solution.py:26
  81.9 157.7 %copy-start.32 = (f32[128,8]{0,1:T(8,128)}, f32[128,8]{0,1:T(8,128)S(1)}, u32[]{:S(2)}) copy-start(f32[128,8]{0,1:T(8,128)S(1)} %copy.171) | copy-start | bytes 12292
  83.3 225.7 %all-gather.15.cloned.1.call-start = ((), (), s32[]{:S(2)}) async-start(), calls=%async_computation.3 | async-start | bytes 4456448 | tf_op jit(solution)/shard_map/all_gather | solution.py:26
  175.8 158.9 %all-gather.11.cloned.1.call-start = ((), (), s32[]{:S(2)}) async-start(), calls=%async_computation.1 | async-start | bytes 4456448 | tf_op jit(solution)/shard_map/all_gather | solution.py:26
  191.9 40.2 %copy-start.8 = (f32[128,128]{1,0:T(8,128)S(1)}, f32[128,128]{1,0:T(8,128)}, u32[]{:S(2)}) copy-start(f32[128,128]{1,0:T(8,128)} %fusion.168) | copy-start | bytes 196612
  191.9 40.2 %copy-start.41 = (f32[1,128,1,64]{1,3,2,0:T(8,128)S(1)}, f32[1,128,1,64]{1,3,2,0:T(8,128)}, u32[]{:S(2)}) copy-start(f32[1,128,1,64]{1,3,2,0:T(8,128)} %slice.377) | copy-start | bytes 98308
  191.9 40.2 %copy-start.52 = (f32[128]{0:T(128)S(1)}, f32[128]{0:T(128)}, u32[]{:S(2)}) copy-start(f32[128]{0:T(128)} %get-tuple-element.811) | copy-start | bytes 1540
  191.9 40.2 %copy-start.54 = (f32[128]{0:T(128)S(1)}, f32[128]{0:T(128)}, u32[]{:S(2)}) copy-start(f32[128]{0:T(128)} %reduce.91) | copy-start | bytes 1540
  191.9 41.2 %copy-start.40 = (f32[1,128,1,64]{1,3,2,0:T(8,128)S(1)}, f32[1,128,1,64]{1,3,2,0:T(8,128)}, u32[]{:S(2)}) copy-start(f32[1,128,1,64]{1,3,2,0:T(8,128)} %slice.381) | copy-start | bytes 98308
  191.9 41.2 %copy-start.62 = (f32[128]{0:T(128)S(1)}, f32[128]{0:T(128)}, u32[]{:S(2)}) copy-start(f32[128]{0:T(128)} %reduce.93) | copy-start | bytes 1540
  191.9 41.2 %copy-start.69 = (f32[128]{0:T(128)S(1)}, f32[128]{0:T(128)}, u32[]{:S(2)}) copy-start(f32[128]{0:T(128)} %get-tuple-element.810) | copy-start | bytes 1540
  191.9 42.1 %copy-start.39 = (f32[1,128,1,64]{1,3,2,0:T(8,128)S(1)}, f32[1,128,1,64]{1,3,2,0:T(8,128)}, u32[]{:S(2)}) copy-start(f32[1,128,1,64]{1,3,2,0:T(8,128)} %slice.385) | copy-start | bytes 98308
  191.9 42.1 %copy-start.61 = (f32[128]{0:T(128)S(1)}, f32[128]{0:T(128)}, u32[]{:S(2)}) copy-start(f32[128]{0:T(128)} %reduce.95) | copy-start | bytes 1540
  192.0 42.1 %copy-start.68 = (f32[128]{0:T(128)S(1)}, f32[128]{0:T(128)}, u32[]{:S(2)}) copy-start(f32[128]{0:T(128)} %get-tuple-element.809) | copy-start | bytes 1540
  192.0 43.0 %copy-start.38 = (f32[1,128,1,64]{1,3,2,0:T(8,128)S(1)}, f32[1,128,1,64]{1,3,2,0:T(8,128)}, u32[]{:S(2)}) copy-start(f32[1,128,1,64]{1,3,2,0:T(8,128)} %slice.389) | copy-start | bytes 98308
  192.0 43.0 %copy-start.60 = (f32[128]{0:T(128)S(1)}, f32[128]{0:T(128)}, u32[]{:S(2)}) copy-start(f32[128]{0:T(128)} %reduce.97) | copy-start | bytes 1540
  192.0 43.0 %copy-start.67 = (f32[128]{0:T(128)S(1)}, f32[128]{0:T(128)}, u32[]{:S(2)}) copy-start(f32[128]{0:T(128)} %get-tuple-element.808) | copy-start | bytes 1540
  192.0 43.9 %copy-start.37 = (f32[1,128,1,64]{1,3,2,0:T(8,128)S(1)}, f32[1,128,1,64]{1,3,2,0:T(8,128)}, u32[]{:S(2)}) copy-start(f32[1,128,1,64]{1,3,2,0:T(8,128)} %slice.393) | copy-start | bytes 98308
  192.0 43.9 %copy-start.59 = (f32[128]{0:T(128)S(1)}, f32[128]{0:T(128)}, u32[]{:S(2)}) copy-start(f32[128]{0:T(128)} %reduce.99) | copy-start | bytes 1540
  192.0 43.9 %copy-start.66 = (f32[128]{0:T(128)S(1)}, f32[128]{0:T(128)}, u32[]{:S(2)}) copy-start(f32[128]{0:T(128)} %get-tuple-element.807) | copy-start | bytes 1540
  192.0 44.8 %copy-start.36 = (f32[1,128,1,64]{1,3,2,0:T(8,128)S(1)}, f32[1,128,1,64]{1,3,2,0:T(8,128)}, u32[]{:S(2)}) copy-start(f32[1,128,1,64]{1,3,2,0:T(8,128)} %slice.397) | copy-start | bytes 98308
  192.0 44.8 %copy-start.58 = (f32[128]{0:T(128)S(1)}, f32[128]{0:T(128)}, u32[]{:S(2)}) copy-start(f32[128]{0:T(128)} %reduce.101) | copy-start | bytes 1540
  192.0 44.8 %copy-start.65 = (f32[128]{0:T(128)S(1)}, f32[128]{0:T(128)}, u32[]{:S(2)}) copy-start(f32[128]{0:T(128)} %get-tuple-element.806) | copy-start | bytes 1540
  192.1 45.7 %copy-start.35 = (f32[1,128,1,64]{1,3,2,0:T(8,128)S(1)}, f32[1,128,1,64]{1,3,2,0:T(8,128)}, u32[]{:S(2)}) copy-start(f32[1,128,1,64]{1,3,2,0:T(8,128)} %slice.401) | copy-start | bytes 98308
  192.1 45.7 %copy-start.57 = (f32[128]{0:T(128)S(1)}, f32[128]{0:T(128)}, u32[]{:S(2)}) copy-start(f32[128]{0:T(128)} %reduce.103) | copy-start | bytes 1540
  192.1 45.7 %copy-start.64 = (f32[128]{0:T(128)S(1)}, f32[128]{0:T(128)}, u32[]{:S(2)}) copy-start(f32[128]{0:T(128)} %get-tuple-element.805) | copy-start | bytes 1540
  192.1 46.6 %copy-start.34 = (f32[1,128,1,64]{1,3,2,0:T(8,128)S(1)}, f32[1,128,1,64]{1,3,2,0:T(8,128)}, u32[]{:S(2)}) copy-start(f32[1,128,1,64]{1,3,2,0:T(8,128)} %slice.405) | copy-start | bytes 98308
  192.1 46.6 %copy-start.56 = (f32[128]{0:T(128)S(1)}, f32[128]{0:T(128)}, u32[]{:S(2)}) copy-start(f32[128]{0:T(128)} %reduce.105) | copy-start | bytes 1540
  192.1 46.6 %copy-start.63 = (f32[128]{0:T(128)S(1)}, f32[128]{0:T(128)}, u32[]{:S(2)}) copy-start(f32[128]{0:T(128)} %get-tuple-element.804) | copy-start | bytes 1540
  339.4 41.8 %copy-start.3 = (f32[1,128,512]{1,2,0:T(8,128)S(1)}, f32[1,128,512]{1,2,0:T(8,128)}, u32[]{:S(2)}) copy-start(f32[1,128,512]{1,2,0:T(8,128)} %copy-done.2) | copy-start | bytes 786436
  382.7 47.0 %copy-start.1 = (f32[1,8,64,128]{3,2,1,0:T(8,128)S(1)}, f32[1,8,64,128]{3,2,1,0:T(8,128)}, u32[]{:S(2)}) copy-start(f32[1,8,64,128]{3,2,1,0:T(8,128)} %copy-done) | copy-start | bytes 786436
  403.1 36.6 %copy-start.6 = (f32[1,128,8]{2,1,0:T(8,128)S(1)}, f32[1,128,8]{2,1,0:T(8,128)}, u32[]{:S(2)}) copy-start(f32[1,128,8]{2,1,0:T(8,128)} %reduce_window_sum.67) | copy-start | bytes 12292
  404.6 35.3 %copy-start.5 = (f32[1,128,8]{2,1,0:T(8,128)S(1)}, f32[1,128,8]{2,1,0:T(8,128)}, u32[]{:S(2)}) copy-start(f32[1,128,8]{2,1,0:T(8,128)} %copy-done.4) | copy-start | bytes 12292
  404.6 35.3 %copy-start.49 = (f32[8]{0:T(128)S(1)}, f32[8]{0:T(128)}, u32[]{:S(2)}) copy-start(f32[8]{0:T(128)} %copy-done.48) | copy-start | bytes 100
  404.6 528.1 %collective-permute-start.5 = (bf16[1,128,768]{2,1,0:T(8,128)(2,1)S(1)}, bf16[1,128,768]{2,1,0:T(8,128)(2,1)S(1)}, u32[]{:S(2)}, u32[]{:S(2)}) collective-permute-start(bf16[1,128,768]{2,1,0:T(8,128)(2,1)S(1)} %get-tuple-element.871), channel_id=1, source_target_pairs={{4,0},{8,4},{12,8},{16,12},{20,16},{24,20},{28,24},{5,1},{9,5},{13... | collective-permute-start | bytes 589832 | tf_op jit(solution)/shard_map/ppermute | solution.py:19
  421.9 510.9 %collective-permute-start.4 = (bf16[1,128,768]{2,1,0:T(8,128)(2,1)S(1)}, bf16[1,128,768]{2,1,0:T(8,128)(2,1)S(1)}, u32[]{:S(2)}, u32[]{:S(2)}) collective-permute-start(bf16[1,128,768]{2,1,0:T(8,128)(2,1)S(1)} %get-tuple-element.871), channel_id=1, source_target_pairs={{0,4},{4,8},{8,12},{12,16},{16,20},{20,24},{24,28},{1,5},{5,9},{9,... | collective-permute-start | bytes 589832 | tf_op jit(solution)/shard_map/ppermute | solution.py:16
  429.4 510.6 %copy-start.13 = (f32[768]{0:T(1024)S(1)}, f32[768]{0:T(1024)}, u32[]{:S(2)}) copy-start(f32[768]{0:T(1024)} %copy-done.12) | copy-start | bytes 9220
  429.4 510.6 %copy-start.15 = (f32[768]{0:T(1024)S(1)}, f32[768]{0:T(1024)}, u32[]{:S(2)}) copy-start(f32[768]{0:T(1024)} %copy-done.14) | copy-start | bytes 9220
  429.4 510.6 %copy-start.17 = (f32[768]{0:T(1024)S(1)}, f32[768]{0:T(1024)}, u32[]{:S(2)}) copy-start(f32[768]{0:T(1024)} %copy-done.16) | copy-start | bytes 9220
  429.4 510.6 %copy-start.19 = (f32[768]{0:T(1024)S(1)}, f32[768]{0:T(1024)}, u32[]{:S(2)}) copy-start(f32[768]{0:T(1024)} %copy-done.18) | copy-start | bytes 9220
  429.4 510.6 %copy-start.21 = (f32[768]{0:T(1024)S(1)}, f32[768]{0:T(1024)}, u32[]{:S(2)}) copy-start(f32[768]{0:T(1024)} %copy-done.20) | copy-start | bytes 9220
  429.4 510.6 %copy-start.23 = (f32[768]{0:T(1024)S(1)}, f32[768]{0:T(1024)}, u32[]{:S(2)}) copy-start(f32[768]{0:T(1024)} %copy-done.22) | copy-start | bytes 9220
  429.4 510.6 %copy-start.25 = (f32[768]{0:T(1024)S(1)}, f32[768]{0:T(1024)}, u32[]{:S(2)}) copy-start(f32[768]{0:T(1024)} %copy-done.24) | copy-start | bytes 9220
  429.5 510.6 %copy-start.27 = (f32[768]{0:T(1024)S(1)}, f32[768]{0:T(1024)}, u32[]{:S(2)}) copy-start(f32[768]{0:T(1024)} %copy-done.26) | copy-start | bytes 9220
  429.5 510.6 %copy-start.29 = (f32[768]{0:T(1024)S(1)}, f32[768]{0:T(1024)}, u32[]{:S(2)}) copy-start(f32[768]{0:T(1024)} %copy-done.28) | copy-start | bytes 9220
  932.8 7.2 collective-permute-start.6
  934.1 5.9 collective-permute-start.7
  (18 other events, 230.6 us)
Sparse Core Ops, SparseCore 0:
  32.0 72.2 all-gather.8
  106.3 74.5 all-gather.12
  183.0 74.6 all-gather.14
  259.6 73.3 all-gather.10
where the time goes:
time: 960 us; the launch traced here: 948 us
  blocking collectives  552 us (58%)
  other arithmetic  135 us (14%)
  matrix products  102 us (11%)
  local copies, waits for them, and re-layouts  99.7 us (10%)
  starting transfers between devices  39.7 us (4%)
  between operations  15.4 us (2%)
    psum x1, blocking collectives, shards(): lax.psum((grad_kernel, grad_rates * rates, jnp.sum(grad_raw, axis=(0, 1))...  489 us
    select_n x90, other arithmetic, step(): jnp.where(position < mine, new, old)  90.8 us
    dot_general x48, matrix products, head_mix(): return jnp.einsum('rij,rjp->rip', mixing, inner_head, precision=PRECISE)  79.5 us
    all_gather x2, blocking collectives, prefix(): pieces = jax.tree.map(lambda part: lax.all_gather(part, axis), value)  48.3 us
    mul x60, local copies, waits for them, and re-layouts, combine(): later[0][..., None, None] * earlier[1] + later[1]  28.7 us
    ppermute x4, starting transfers between devices, extended(): lax.ppermute(lax.slice_in_dim(block, 0, width, axis=dim), axis, backward)  28.6 us
    broadcast_in_dim x16, local copies, waits for them, and re-layouts, block_mix(): step_sizes[:, :, member]  21.9 us
  transfers between devices with their start and end apart: 12, of which 1 were waited for; matrix products, arithmetic and copies ran while one was open for 29% of the time, Pallas kernels for 0%

commit v1 on v0

v1 whole, which is shorter than its diff:
```python
from functools import partial

import jax
import jax.numpy as jnp
from jax import lax
from jax.experimental import pallas as pl
from jax.experimental.pallas import tpu as pltpu
from jax.sharding import PartitionSpec as P

MESH = pl.DeviceIdType.MESH
F32 = jnp.float32
BF16 = jnp.bfloat16
T = 128
EXT = T + 16
EDGES = ((0, -1), (0, 1), (-1, -1), (-1, 1), (1, -1), (1, 1))


def hi(a, b):
    return jnp.dot(a, b, precision=lax.Precision.HIGHEST, preferred_element_type=F32)


def nn(a, b):
    return jnp.dot(a, b, preferred_element_type=F32)


def nt(a, b):
    return lax.dot_general(a, b, (((1,), (1,)), ((), ())), preferred_element_type=F32)


def tn(a, b):
    return lax.dot_general(a, b, (((0,), (0,)), ((), ())), preferred_element_type=F32)


def grid_peer(d_lat, d_lon):
    lat_n, lon_n = lax.axis_size("lat"), lax.axis_size("lon")
    return {
        "lat": lax.rem(lax.axis_index("lat") + d_lat + lat_n, lat_n),
        "lon": lax.rem(lax.axis_index("lon") + d_lon + lon_n, lon_n),
    }


def greet(peers):
    barrier = pltpu.get_barrier_semaphore()
    for peer in peers:
        pl.semaphore_signal(barrier, inc=1, device_id=peer, device_id_type=MESH)
    pl.semaphore_wait(barrier, len(peers))


def grid_peers():
    return [grid_peer(a, b) for a in (-1, 0, 1) for b in (-1, 0, 1) if (a, b) != (0, 0)]


def halo_copies(src, rows, edges, send, recv):
    copies = []
    for slot, a in enumerate((-1, 1)):
        copies.append(
            pltpu.make_async_remote_copy(
                src, rows.at[slot], send.at[slot], recv.at[slot],
                device_id=grid_peer(-a, 0), device_id_type=MESH,
            )
        )
    for slot, (a, b) in enumerate(EDGES):
        part = src.at[pl.ds(T - 16, 16)] if b < 0 else src.at[pl.ds(0, 16)]
        copies.append(
            pltpu.make_async_remote_copy(
                part, edges.at[slot], send.at[2 + slot], recv.at[2 + slot],
                device_id=grid_peer(-a, -b), device_id_type=MESH,
            )
        )
    return copies


def fill_extended(src, rows, edges, ext):
    lat, lon = lax.axis_index("lat"), lax.axis_index("lon")
    lat_n, lon_n = lax.axis_size("lat"), lax.axis_size("lon")
    keep = {
        (1, -1): (lat > 0).astype(F32),
        (1, 1): (lat < lat_n - 1).astype(F32),
        (2, -1): (lon > 0).astype(F32),
        (2, 1): (lon < lon_n - 1).astype(F32),
    }
    ext[1, 8 : 8 + T] = src[...].astype(F32)
    ext[0, 8 : 8 + T] = rows[0].astype(F32) * keep[1, -1]
    ext[2, 8 : 8 + T] = rows[1].astype(F32) * keep[1, 1]
    for slot, (a, b) in enumerate(EDGES):
        scale = keep[2, b] if a == 0 else keep[2, b] * keep[1, a]
        tile = edges[slot].astype(F32) * scale
        if b < 0:
            ext[a + 1, 0:8] = tile[8:16]
        else:
            ext[a + 1, 8 + T :] = tile[0:8]


def stencil(ext, taps, lanes, adjoint):
    sums = []
    for b in range(3):
        total = None
        for a in range(3):
            term = taps[3 * a + b : 3 * a + b + 1, lanes] * ext[2 - a if adjoint else a, :, lanes]
            total = term if total is None else total + term
        sums.append(total)
    west, east = (sums[2], sums[0]) if adjoint else (sums[0], sums[2])
    full = pltpu.roll(west, 1, 0) + sums[1] + pltpu.roll(east, EXT - 1, 0)
    return full[8 : 8 + T]


def conv_kernel(joined, taps, before, active, ext, rows, edges, send, recv):
    greet(grid_peers())
    copies = halo_copies(joined, rows, edges, send, recv)
    for copy in copies:
        copy.start()
    for copy in copies:
        copy.wait()
    fill_extended(joined, rows, edges, ext)
    for part in range(joined.shape[1] // 128):
        lanes = slice(128 * part, 128 * part + 128)
        value = stencil(ext, taps, lanes, False)
        before[:, lanes] = value
        active[:, lanes] = (value * jax.nn.sigmoid(value)).astype(BF16)


def adjoint_kernel(grad, taps, out_f, out_p, ext, rows, edges, send, recv):
    greet(grid_peers())
    copies = halo_copies(grad, rows, edges, send, recv)
    for copy in copies:
        copy.start()
    for copy in copies:
        copy.wait()
    fill_extended(grad, rows, edges, ext)
    width = out_f.shape[1]
    for part in range(grad.shape[1] // 128):
        lanes = slice(128 * part, 128 * part + 128)
        value = stencil(ext, taps, lanes, True).astype(BF16)
        if 128 * part < width:
            out_f[:, lanes] = value
        else:
            out_p[:, 128 * part - width : 128 * part - width + 128] = value


def state_kernel(
    active, before, ext, cot, raw_c, raw_r, bias_r, bias_c, logs_r, logs_c, gain, start_e, start_w,
    mixed, grad_before, grad_step, params,
    add_r, add_l, in_r, in_l, out_r, out_l, dec_r, dec_l, cols, gathered,
    send_r, recv_r, send_l, recv_l, send_t, recv_t,
):
    lon, tp = lax.axis_index("lon"), lax.axis_index("tp")
    lon_n, tp_n = lax.axis_size("lon"), lax.axis_size("tp")
    heads = raw_c.shape[1]
    width = cot.shape[1]
    size = width // heads
    chunks = 2 * heads
    tp_peers = [{"tp": lax.rem(tp + d, tp_n)} for d in range(1, tp_n)]
    greet([grid_peer(0, -1), grid_peer(0, 1)] + tp_peers)

    row_i = lax.broadcasted_iota(jnp.int32, (T, T), 0)
    col_i = lax.broadcasted_iota(jnp.int32, (T, T), 1)
    lower = (row_i >= col_i).astype(F32)
    upper = (row_i <= col_i).astype(F32)
    spread = (
        lax.broadcasted_iota(jnp.int32, (heads, width), 1) // size
        == lax.broadcasted_iota(jnp.int32, (heads, width), 0)
    ).astype(F32)
    gather = (
        lax.broadcasted_iota(jnp.int32, (width, heads), 0) // size
        == lax.broadcasted_iota(jnp.int32, (width, heads), 1)
    ).astype(F32)

    def softplus(v):
        return jnp.maximum(v, 0.0) + jnp.log1p(jnp.exp(-jnp.abs(v)))

    shifted = raw_c[...] + bias_r[...]
    steps = softplus(shifted)
    steps_r = softplus(raw_r[...] + bias_c[...])
    rate_e, rate_w = jnp.exp(logs_r[0:1]), jnp.exp(logs_r[1:2])
    rates_c = jnp.exp(logs_c[...])
    sum_e = hi(lower, -steps * rate_e)
    sum_w = hi(upper, -steps * rate_w)
    sum_er = hi(-steps_r * rates_c[:, 0:1], upper)
    sum_wr = hi(-steps_r * rates_c[:, 1:2], lower)
    tot_e, tot_w = sum_e[T - 1 : T], sum_w[0:1]
    far_e, far_w = jnp.exp(tot_e - sum_e), jnp.exp(tot_w - sum_w)
    fac_e, fac_w = far_e * steps, far_w * steps
    wide_ee, wide_ew = hi(jnp.exp(sum_e), spread), hi(jnp.exp(sum_w), spread)
    wide_fe, wide_fw = hi(fac_e, spread), hi(fac_w, spread)
    close_e = jnp.broadcast_to(jnp.exp(sum_er[:, T - 1 : T]), (heads, T))
    close_w = jnp.broadcast_to(jnp.exp(sum_wr[:, 0:1]), (heads, T))
    dec_r[0:heads] = close_e
    dec_r[heads:chunks] = close_w
    dec_l[0:heads] = close_w
    dec_l[heads:chunks] = close_e

    inner = active[:, 0:width].astype(F32)
    b_part = active[:, width : width + T]
    c_part = active[:, width + T : width + 2 * T]
    incoming = cot[...].astype(F32)
    src_e, src_w = (inner * wide_fe).astype(BF16), (inner * wide_fw).astype(BF16)
    inc_e, inc_w = (incoming * wide_ee).astype(BF16), (incoming * wide_ew).astype(BF16)
    shape3 = (heads, size, T)
    add_r[0:heads] = tn(src_e, b_part).reshape(shape3)
    add_r[heads:chunks] = tn(inc_w, c_part).reshape(shape3)
    add_l[0:heads] = tn(src_w, b_part).reshape(shape3)
    add_l[heads:chunks] = tn(inc_e, c_part).reshape(shape3)

    @pl.when(lon == 0)
    def _():
        in_r[0:heads] = start_e[...].reshape(shape3)
        in_r[heads:chunks] = jnp.zeros(shape3, F32)

    @pl.when(lon == lon_n - 1)
    def _():
        in_l[0:heads] = start_w[...].reshape(shape3)
        in_l[heads:chunks] = jnp.zeros(shape3, F32)

    def copy_r(q):
        return pltpu.make_async_remote_copy(
            out_r.at[q], in_r.at[q], send_r.at[q], recv_r.at[q],
            device_id=grid_peer(0, 1), device_id_type=MESH,
        )

    def copy_l(q):
        return pltpu.make_async_remote_copy(
            out_l.at[q], in_l.at[q], send_l.at[q], recv_l.at[q],
            device_id=grid_peer(0, -1), device_id_type=MESH,
        )

    lead = 3
    skew_r = jnp.maximum(0, (2 * lon - (lon_n - 1)) * lead)
    skew_l = jnp.maximum(0, ((lon_n - 1) - 2 * lon) * lead)

    def hop(slot, _):
        q_r, q_l = slot - skew_r, slot - skew_l

        @pl.when((q_r >= 0) & (q_r < chunks))
        def _():
            @pl.when(lon > 0)
            def _():
                copy_r(q_r).wait_recv()

            @pl.when(lon < lon_n - 1)
            def _():
                out_r[q_r] = dec_r[pl.ds(q_r, 1), :] * in_r[q_r] + add_r[q_r]
                copy_r(q_r).start()

        @pl.when((q_l >= 0) & (q_l < chunks))
        def _():
            @pl.when(lon < lon_n - 1)
            def _():
                copy_l(q_l).wait_recv()

            @pl.when(lon > 0)
            def _():
                out_l[q_l] = dec_l[pl.ds(q_l, 1), :] * in_l[q_l] + add_l[q_l]
                copy_l(q_l).start()

        return 0

    lax.fori_loop(0, chunks + lead * (lon_n - 1), hop, 0)

    scores = nt(c_part, b_part)
    head_i = lax.broadcasted_iota(jnp.int32, (T, heads), 1)
    lane_half = lax.broadcasted_iota(jnp.int32, (T, T), 1) // size
    row_l = jnp.zeros((T, heads), F32)
    row_u = jnp.zeros((T, heads), F32)
    grad_scores = jnp.zeros((T, T), F32)
    per = T // size
    mixes, pulls = [], []
    for pair in range(heads // per):
        lanes = slice(T * pair, T * pair + T)
        inner_p, incoming_p = inner[:, lanes], incoming[:, lanes]
        mix, pull = None, None
        for member in range(per):
            h = per * pair + member
            mine = (lane_half == member).astype(F32)
            inner_m = (inner_p * mine).astype(BF16)
            incoming_m = (incoming_p * mine).astype(BF16)
            gap = jnp.where(
                row_i >= col_i,
                sum_e[:, h : h + 1] - sum_er[h : h + 1],
                sum_w[:, h : h + 1] - sum_wr[h : h + 1],
            )
            decay = jnp.where(row_i == col_i, 2.0, jnp.exp(gap)) * steps_r[h : h + 1]
            grad_mix = nt(incoming_m, inner_m) * decay
            grad_scores = grad_scores + grad_mix
            weight = grad_mix * scores
            below = jnp.where(row_i > col_i, weight, 0.0)
            above = jnp.where(row_i < col_i, weight, 0.0)
            row_l = jnp.where(head_i == h, jnp.sum(below, axis=1, keepdims=True), row_l)
            row_u = jnp.where(head_i == h, jnp.sum(above, axis=1, keepdims=True), row_u)
            cols[0, h : h + 1] = jnp.sum(below, axis=0, keepdims=True)
            cols[1, h : h + 1] = jnp.sum(above, axis=0, keepdims=True)
            cols[2, h : h + 1] = jnp.sum(weight, axis=0, keepdims=True)
            mixing = (decay * scores).astype(BF16)
            y, g = nn(mixing, inner_m), tn(mixing, incoming_m)
            mix = y if mix is None else mix + y
            pull = g if pull is None else pull + g
        mixes.append(mix)
        pulls.append(pull)
    grad_inner = jnp.concatenate(pulls, axis=1)
    total = jnp.concatenate(mixes, axis=1)

    def settle(q, _):
        @pl.when(lon < lon_n - 1)
        def _():
            copy_r(q).wait_send()

        @pl.when(lon > 0)
        def _():
            copy_l(q).wait_send()

        return 0

    lax.fori_loop(0, chunks, settle, 0)

    flat = (width, T)
    ent_e, adj_w = in_r[0:heads].reshape(flat), in_r[heads:chunks].reshape(flat)
    ent_w, adj_e = in_l[0:heads].reshape(flat), in_l[heads:chunks].reshape(flat)
    ent_eb, ent_wb = ent_e.astype(BF16), ent_w.astype(BF16)
    adj_eb, adj_wb = adj_e.astype(BF16), adj_w.astype(BF16)

    scores_b = grad_scores.astype(BF16)
    me = pl.ds(tp, 1)
    grad_b = tn(scores_b, c_part) + nn(src_e, adj_eb) + nn(src_w, adj_wb)
    grad_c = nn(scores_b, b_part) + nn(inc_e, ent_eb) + nn(inc_w, ent_wb)
    gathered[me, :, 0:T] = grad_b[None]
    gathered[me, :, T : 2 * T] = grad_c[None]
    copies = [
        pltpu.make_async_remote_copy(
            gathered.at[tp], gathered.at[tp], send_t.at[d], recv_t.at[d],
            device_id=peer, device_id_type=MESH,
        )
        for d, peer in enumerate(tp_peers)
    ]
    for copy in copies:
        copy.start()

    read_e = nt(c_part, ent_eb) * wide_ee
    read_w = nt(c_part, ent_wb) * wide_ew
    pull_e, pull_w = nt(b_part, adj_eb), nt(b_part, adj_wb)
    mixed[...] = (total + read_e + read_w + gain[...] * inner).astype(BF16)
    grad_inner = grad_inner + wide_fe * pull_e + wide_fw * pull_w + gain[...] * incoming
    r_e, r_w = hi(read_e * incoming, gather), hi(read_w * incoming, gather)
    q_e, q_w = hi(pull_e * inner, gather), hi(pull_w * inner, gather)
    ones = jnp.ones((8, T), F32)

    def per_head(v):
        return lax.dot_general(
            ones, hi(spread, v), (((1,), (1,)), ((), ())),
            precision=lax.Precision.HIGHEST, preferred_element_type=F32,
        )[0:1]

    end_e, end_w = per_head(adj_e * ent_e), per_head(adj_w * ent_w)
    w_e, w_w = fac_e * q_e, fac_w * q_w
    const_e = jnp.sum(w_e, axis=0, keepdims=True) + jnp.exp(tot_e) * end_e
    const_w = jnp.sum(w_w, axis=0, keepdims=True) + jnp.exp(tot_w) * end_w
    grad_log_e = hi(upper, row_l - cols[0].T + r_e - w_e) + const_e
    grad_log_w = hi(lower, row_u - cols[1].T + r_w - w_w) + const_w
    grad_steps = (
        (cols[2] / steps_r).T + far_e * q_e + far_w * q_w - rate_e * grad_log_e - rate_w * grad_log_w
    )
    grad_raw = grad_steps * jax.nn.sigmoid(shifted)
    grad_step[...] = grad_raw
    params[...] = jnp.zeros(params.shape, F32)
    params[9:10, 0:heads] = jnp.sum(-steps * rate_e * grad_log_e, axis=0, keepdims=True)
    params[10:11, 0:heads] = jnp.sum(-steps * rate_w * grad_log_w, axis=0, keepdims=True)
    params[11:12, 0:heads] = jnp.sum(grad_raw, axis=0, keepdims=True)
    params[12:13, 0:heads] = jnp.sum(hi(incoming * inner, gather), axis=0, keepdims=True)

    def back(lanes, grad_active):
        value = before[:, lanes]
        slope = jax.nn.sigmoid(value)
        grad = (
            grad_active.astype(BF16).astype(F32) * slope * (1.0 + value * (1.0 - slope))
        ).astype(BF16)
        grad_before[:, lanes] = grad
        edge = jnp.zeros((8, 128), F32)
        wide = jnp.concatenate([edge, grad.astype(F32), edge], axis=0)
        for b in range(3):
            moved = wide if b == 1 else pltpu.roll(wide, EXT - 1 if b == 0 else 1, 0)
            for a in range(3):
                params[3 * a + b : 3 * a + b + 1, lanes] = jnp.sum(
                    moved * ext[a, :, lanes], axis=0, keepdims=True
                )

    for part in range(width // 128):
        lanes = slice(128 * part, 128 * part + 128)
        back(lanes, grad_inner[:, lanes])
    for copy in copies:
        copy.wait()
    proj = gathered[0]
    for d in range(1, tp_n):
        proj = proj + gathered[d]
    for part in range(2):
        back(slice(width + 128 * part, width + 128 * part + 128), proj[:, 128 * part : 128 * part + 128])


VM = pl.BlockSpec(memory_space=pltpu.VMEM)


def call(kernel, outs, scratch, ident, ins):
    return pl.pallas_call(
        kernel,
        out_shape=outs,
        in_specs=[VM] * len(ins),
        out_specs=tuple(VM for _ in outs),
        scratch_shapes=scratch,
        compiler_params=pltpu.CompilerParams(
            collective_id=ident, has_side_effects=True, vmem_limit_bytes=60 << 20
        ),
    )(*ins)


def shards(
    features, projections, step_raw, step_bias, decay_log, skip_gain, conv_features,
    conv_projections, state_east, state_west, cotangent,
):
    width, heads = features.shape[2], step_raw.shape[2]
    both = width + projections.shape[2]
    tp_n = lax.axis_size("tp")
    sds = jax.ShapeDtypeStruct
    dma = pltpu.SemaphoreType.DMA
    joined = jnp.concatenate([features[0], projections[0]], axis=1)
    taps = jnp.concatenate([conv_features, conv_projections], axis=1)
    halo = [
        pltpu.VMEM((2, T, both), BF16),
        pltpu.VMEM((6, 16, both), BF16),
        dma((8,)),
        dma((8,)),
    ]
    ext_shape = (3, EXT, both)
    before, active, ext = call(
        conv_kernel,
        (sds((T, both), F32), sds((T, both), BF16), sds(ext_shape, F32)),
        halo,
        0,
        (joined, taps),
    )
    raw = step_raw[0]
    flat = (width, T)
    chunks = 2 * heads
    block = pltpu.VMEM((chunks, width // heads, T), F32)
    mixed, grad_before, grad_step, params = call(
        state_kernel,
        (sds((T, width), BF16), sds((T, both), BF16), sds((T, heads), F32), sds((16, both), F32)),
        [
            block, block, block, block, block, block,
            pltpu.VMEM((chunks, T), F32),
            pltpu.VMEM((chunks, T), F32),
            pltpu.VMEM((3, heads, T), F32),
            pltpu.VMEM((tp_n, T, both - width), F32),
            dma((chunks,)), dma((chunks,)), dma((chunks,)), dma((chunks,)),
            dma((tp_n - 1,)), dma((tp_n - 1,)),
        ],
        1,
        (
            active, before, ext, cotangent[0], raw, raw.T, step_bias[None], step_bias[:, None],
            decay_log, decay_log.T, jnp.repeat(skip_gain, width // heads)[None],
            state_east.reshape(flat), state_west.reshape(flat),
        ),
    )
    totals = lax.psum(params, ("lon", "lat"))
    grad_f, grad_p = call(
        adjoint_kernel,
        (sds((T, width), BF16), sds((T, both - width), BF16)),
        [pltpu.VMEM(ext_shape, F32)] + halo,
        2,
        (grad_before, taps),
    )
    cells = T * lax.axis_size("lat") * lax.axis_size("lon")
    totals = totals * cells ** (-0.5)
    return (
        mixed[None], grad_f[None], grad_p[None], grad_step[None],
        totals[0:9, :width], totals[0:9, width:], totals[9:11, :heads],
        totals[11, :heads], totals[12, :heads],
    )


def solution(mesh):
    in_specs = (
        P("lat", "lon", "tp"),
        P("lat", "lon", None),
        P("lat", "lon", "tp"),
        P("tp"),
        P(None, "tp"),
        P("tp"),
        P(None, "tp"),
        P(),
        P("lat", "tp", None, None),
        P("lat", "tp", None, None),
        P("lat", "lon", "tp"),
    )
    out_specs = (
        P("lat", "lon", "tp"),
        P("lat", "lon", "tp"),
        P("lat", "lon", None),
        P("lat", "lon", "tp"),
        P(None, "tp"),
        P(),
        P(None, "tp"),
        P("tp"),
        P("tp"),
    )
    return jax.shard_map(shards, mesh=mesh, in_specs=in_specs, out_specs=out_specs, check_vma=False)
```

time: 960 us -> 617 us (0.64); the launches traced: 948 us -> 616 us
  other arithmetic: 135 us -> 1.63 us
  matrix products: 102 us -> 0 us
  Pallas kernels: 0 us -> 95 us
  local copies, waits for them, and re-layouts: 99.7 us -> 15.4 us
  blocking collectives: 552 us -> 503 us
  starting transfers between devices: 39.7 us -> 0 us
  between operations: 15.4 us -> 0.68 us
    dot_general x66 -> x0, matrix products: 102 us -> none  [the longest x48 79.5 us: head_mix(): return jnp.einsum('rij,rjp->rip', mixing, inner_head, precision=PRECISE)]
    pallas_call x0 -> x3, Pallas kernels: none -> 95 us  [call(): pl.pallas_call(kernel, out_shape=outs, in_specs=[VM] * len(ins), out_spec...]
    select_n x90 -> x0, other arithmetic: 90.8 us -> none  [step(): jnp.where(position < mine, new, old)]
    all_gather x2 -> x0, blocking collectives: 48.3 us -> none  [prefix(): pieces = jax.tree.map(lambda part: lax.all_gather(part, axis), value)]
    ppermute x8 -> x0, starting transfers between devices: 39.3 us -> none  [the longest x4 28.6 us: extended(): lax.ppermute(lax.slice_in_dim(block, 0, width, axis=dim), axis, backward)]
    mul x69 -> x0, local copies, waits for them, and re-layouts: 29.4 us -> none  [the longest x60 28.7 us: combine(): later[0][..., None, None] * earlier[1] + later[1]]
    reduce_sum x22 -> x0, other arithmetic: 20.5 us -> none  [the longest x8 6.93 us: head_mix(): decay_head[:, :, None] - decay_head[:, None, :]]
    broadcast_in_dim x16 -> x2, local copies, waits for them, and re-layouts: 21.9 us -> 2.05 us  [the longest x1 1.32 us: shards(): step_bias[:, None]]
  transfers between devices with their start and end apart: 12 -> 0, of which waited for: 1 -> 0; matrix products, arithmetic and copies ran while one was open for 29% -> 0% of each run, Pallas kernels for 0% -> 0%
where the time goes in v1:
time: 617 us; the launch traced here: 616 us
  blocking collectives  503 us (82%)
  Pallas kernels  95 us (15%)
  local copies, waits for them, and re-layouts  15.4 us (2%)
    psum x1, blocking collectives, shards(): totals = lax.psum(params, ('lon', 'lat'))  503 us
    pallas_call x3, Pallas kernels, call(): pl.pallas_call(kernel, out_shape=outs, in_specs=[VM] * len(ins), out_spec...  95 us

profile of v1, /device:TPU:1, one launch (start us, length us, event | category | flops | bytes accessed | tf_op | source)
XLA Modules:
  0.0 616.0 jit_solution(4227242507588183876)
XLA Ops:
  0.6 0.7 broadcast_in_dim.23
  1.4 0.7 broadcast_in_dim_reshape.3.gain
  2.0 1.3 copy.22.bias_c
  3.3 1.3 copy.20
  4.7 0.8 constant_dynamic-update-slice_fusion.1
  5.4 0.7 constant_dynamic-update-slice_fusion.taps
  6.2 0.0 copy-start
  6.2 1.4 copy.21.raw_c
  7.6 1.6 pad_maximum_fusion.joined
  9.2 0.0 copy-done
  9.2 19.6 %shard_map.178 = (f32[128,768]{1,0:T(8,128)}, bf16[128,768]{1,0:T(8,128)(2,1)}, f32[3,144,768]{2,1,0:T(8,128)}) custom-call(bf16[128,768]{1,0:T(8,128)(2,1)} %pad_maximum_fusion.joined, f32[9,768]{1,0:T(8,128)} %copy-done), custom_call_target="tpu_custom_call" | custom-call | tf_op jit(solution)/shard_map/pallas_call | solution.py:400
  28.8 61.9 %shard_map.179 = (bf16[128,512]{1,0:T(8,128)(2,1)}, bf16[128,768]{1,0:T(8,128)(2,1)}, f32[128,8]{1,0:T(8,128)}, f32[16,768]{1,0:T(8,128)}) custom-call(bf16[128,768]{1,0:T(8,128)(2,1)} %get-tuple-element.18.active, f32[128,768]{1,0:T(8,128)} %get-tuple-element.19.before, f32[3,144,768]{2,1,0:T(8,128)} %get-tuple-element.20.ext, bf16[128,512]{1,0:T(8,128)(2,1)} %bitcast.22, ...), custom_call_target="tpu_custom_call" | custom-call | tf_op jit(solution)/shard_map/pallas_call | solution.py:400
  90.7 1.5 copy.23
  92.2 503.3 %psum.7 = f32[16,768]{1,0:T(8,128)S(1)} all-reduce(f32[16,768]{1,0:T(8,128)} %get-tuple-element.26), channel_id=1, replica_groups=mesh['lon'=16,'lat'=8,'tp'=4] {'lon','lat'}, use_global_device_ids=true, to_apply=%region_0.0 | all-reduce | flops 12288 | bytes 98304 | tf_op jit(solution)/shard_map/psum | solution.py:460
  595.6 0.6 slice.22
  596.2 0.5 slice_bitcast_fusion
  596.7 0.6 slice.21
  597.3 0.6 slice.20
  597.9 13.5 %shard_map.180 = (bf16[128,512]{1,0:T(8,128)(2,1)}, bf16[128,256]{1,0:T(8,128)(2,1)}) custom-call(bf16[128,768]{1,0:T(8,128)(2,1)} %get-tuple-element.22.grad, f32[9,768]{1,0:T(8,128)} %copy-done), custom_call_target="tpu_custom_call" | custom-call | tf_op jit(solution)/shard_map/pallas_call | solution.py:400
  611.4 1.6 copy.28
  613.0 1.6 copy.29
  614.6 1.5 copy.30
  (1 shorter events, 0.0 us)
Async XLA Ops:
  6.2 3.1 copy-start

commit v2 on v1

--- a/solution.py
+++ b/solution.py
@@ -50,12 +50,12 @@
     return [grid_peer(a, b) for a in (-1, 0, 1) for b in (-1, 0, 1) if (a, b) != (0, 0)]
 
 
-def halo_copies(src, rows, edges, send, recv):
+def halo_copies(src, lanes, rows, edges, send, recv, base):
     copies = []
     for slot, a in enumerate((-1, 1)):
         copies.append(
             pltpu.make_async_remote_copy(
-                src, rows.at[slot], send.at[slot], recv.at[slot],
+                src, rows.at[slot, :, lanes], send.at[base + slot], recv.at[base + slot],
                 device_id=grid_peer(-a, 0), device_id_type=MESH,
             )
         )
@@ -63,14 +63,14 @@
         part = src.at[pl.ds(T - 16, 16)] if b < 0 else src.at[pl.ds(0, 16)]
         copies.append(
             pltpu.make_async_remote_copy(
-                part, edges.at[slot], send.at[2 + slot], recv.at[2 + slot],
+                part, edges.at[slot, :, lanes], send.at[base + 2 + slot], recv.at[base + 2 + slot],
                 device_id=grid_peer(-a, -b), device_id_type=MESH,
             )
         )
     return copies
 
 
-def fill_extended(src, rows, edges, ext):
+def fill_extended(own, lanes, rows, edges, ext):
     lat, lon = lax.axis_index("lat"), lax.axis_index("lon")
     lat_n, lon_n = lax.axis_size("lat"), lax.axis_size("lon")
     keep = {
@@ -79,16 +79,16 @@
         (2, -1): (lon > 0).astype(F32),
         (2, 1): (lon < lon_n - 1).astype(F32),
     }
-    ext[1, 8 : 8 + T] = src[...].astype(F32)
-    ext[0, 8 : 8 + T] = rows[0].astype(F32) * keep[1, -1]
-    ext[2, 8 : 8 + T] = rows[1].astype(F32) * keep[1, 1]
+    ext[1, 8 : 8 + T, lanes] = own.astype(F32)
+    ext[0, 8 : 8 + T, lanes] = rows[0, :, lanes].astype(F32) * keep[1, -1]
+    ext[2, 8 : 8 + T, lanes] = rows[1, :, lanes].astype(F32) * keep[1, 1]
     for slot, (a, b) in enumerate(EDGES):
         scale = keep[2, b] if a == 0 else keep[2, b] * keep[1, a]
-        tile = edges[slot].astype(F32) * scale
+        tile = edges[slot, :, lanes].astype(F32) * scale
         if b < 0:
-            ext[a + 1, 0:8] = tile[8:16]
+            ext[a + 1, 0:8, lanes] = tile[8:16]
         else:
-            ext[a + 1, 8 + T :] = tile[0:8]
+            ext[a + 1, 8 + T :, lanes] = tile[0:8]
 
 
 def stencil(ext, taps, lanes, adjoint):
@@ -104,53 +104,35 @@
     return full[8 : 8 + T]
 
 
-def conv_kernel(joined, taps, before, active, ext, rows, edges, send, recv):
-    greet(grid_peers())
-    copies = halo_copies(joined, rows, edges, send, recv)
-    for copy in copies:
-        copy.start()
-    for copy in copies:
-        copy.wait()
-    fill_extended(joined, rows, edges, ext)
-    for part in range(joined.shape[1] // 128):
-        lanes = slice(128 * part, 128 * part + 128)
-        value = stencil(ext, taps, lanes, False)
-        before[:, lanes] = value
-        active[:, lanes] = (value * jax.nn.sigmoid(value)).astype(BF16)
-
-
-def adjoint_kernel(grad, taps, out_f, out_p, ext, rows, edges, send, recv):
-    greet(grid_peers())
-    copies = halo_copies(grad, rows, edges, send, recv)
-    for copy in copies:
-        copy.start()
-    for copy in copies:
-        copy.wait()
-    fill_extended(grad, rows, edges, ext)
-    width = out_f.shape[1]
-    for part in range(grad.shape[1] // 128):
-        lanes = slice(128 * part, 128 * part + 128)
-        value = stencil(ext, taps, lanes, True).astype(BF16)
-        if 128 * part < width:
-            out_f[:, lanes] = value
-        else:
-            out_p[:, 128 * part - width : 128 * part - width + 128] = value
-
-
-def state_kernel(
-    active, before, ext, cot, raw_c, raw_r, bias_r, bias_c, logs_r, logs_c, gain, start_e, start_w,
-    mixed, grad_before, grad_step, params,
+def layer_kernel(
+    features, projections, cot, raw_r, bias_r, logs_r, gain_r, taps_f, taps_p, start_e, start_w,
+    mixed, out_f, out_p, grad_step, out_taps_f, out_taps_p, out_logs, out_bias, out_gain,
+    before, active, ext, ext_g, grad_before, taps, rows, edges, rows_g, edges_g,
     add_r, add_l, in_r, in_l, out_r, out_l, dec_r, dec_l, cols, gathered,
-    send_r, recv_r, send_l, recv_l, send_t, recv_t,
+    params, by_lat, by_lon, whole,
+    send_h, recv_h, send_g, recv_g, send_r, recv_r, send_l, recv_l, send_t, recv_t,
+    send_a, recv_a, send_b, recv_b, send_c, recv_c,
 ):
-    lon, tp = lax.axis_index("lon"), lax.axis_index("tp")
-    lon_n, tp_n = lax.axis_size("lon"), lax.axis_size("tp")
-    heads = raw_c.shape[1]
+    lon, tp, lat = lax.axis_index("lon"), lax.axis_index("tp"), lax.axis_index("lat")
+    lon_n, tp_n, lat_n = lax.axis_size("lon"), lax.axis_size("tp"), lax.axis_size("lat")
+    heads = raw_r.shape[0]
     width = cot.shape[1]
+    both = width + projections.shape[1]
     size = width // heads
     chunks = 2 * heads
     tp_peers = [{"tp": lax.rem(tp + d, tp_n)} for d in range(1, tp_n)]
-    greet([grid_peer(0, -1), grid_peer(0, 1)] + tp_peers)
+    lat_others = [lax.rem(lat + d, lat_n) for d in range(1, lat_n)]
+    lon_others = [lax.rem(lon + d, lon_n) for d in range(1, lon_n)]
+    greet(
+        grid_peers() + tp_peers + [{"lat": o} for o in lat_others] + [{"lon": o} for o in lon_others]
+    )
+    lanes_f, lanes_p = pl.ds(0, width), pl.ds(width, both - width)
+    halo = halo_copies(features, lanes_f, rows, edges, send_h, recv_h, 0)
+    halo += halo_copies(projections, lanes_p, rows, edges, send_h, recv_h, 8)
+    for copy in halo:
+        copy.start()
+    taps[:, 0:width] = taps_f[...]
+    taps[:, width:both] = taps_p[...]
 
     row_i = lax.broadcasted_iota(jnp.int32, (T, T), 0)
     col_i = lax.broadcasted_iota(jnp.int32, (T, T), 1)
@@ -168,15 +150,13 @@
     def softplus(v):
         return jnp.maximum(v, 0.0) + jnp.log1p(jnp.exp(-jnp.abs(v)))
 
-    shifted = raw_c[...] + bias_r[...]
+    shifted = raw_r[...].T + bias_r[...]
     steps = softplus(shifted)
-    steps_r = softplus(raw_r[...] + bias_c[...])
+    steps_r = steps.T
     rate_e, rate_w = jnp.exp(logs_r[0:1]), jnp.exp(logs_r[1:2])
-    rates_c = jnp.exp(logs_c[...])
     sum_e = hi(lower, -steps * rate_e)
     sum_w = hi(upper, -steps * rate_w)
-    sum_er = hi(-steps_r * rates_c[:, 0:1], upper)
-    sum_wr = hi(-steps_r * rates_c[:, 1:2], lower)
+    sum_er, sum_wr = sum_e.T, sum_w.T
     tot_e, tot_w = sum_e[T - 1 : T], sum_w[0:1]
     far_e, far_w = jnp.exp(tot_e - sum_e), jnp.exp(tot_w - sum_w)
     fac_e, fac_w = far_e * steps, far_w * steps
@@ -189,6 +169,21 @@
     dec_l[0:heads] = close_w
     dec_l[heads:chunks] = close_e
 
+    gain = hi(jnp.broadcast_to(gain_r[...], (8, heads)), spread)[0:1]
+
+    for copy in halo:
+        copy.wait()
+    for part in range(both // 128):
+        lanes = slice(128 * part, 128 * part + 128)
+        if 128 * part < width:
+            own = features[:, lanes]
+        else:
+            own = projections[:, 128 * part - width : 128 * part - width + 128]
+        fill_extended(own, lanes, rows, edges, ext)
+        value = stencil(ext, taps, lanes, False)
+        before[:, lanes] = value
+        active[:, lanes] = (value * jax.nn.sigmoid(value)).astype(BF16)
+
     inner = active[:, 0:width].astype(F32)
     b_part = active[:, width : width + T]
     c_part = active[:, width + T : width + 2 * T]
@@ -254,7 +249,10 @@
 
         return 0
 
-    lax.fori_loop(0, chunks + lead * (lon_n - 1), hop, 0)
+    slots = chunks + lead * (lon_n - 1)
+    idle = (skew_r >= lead * 10) | (skew_l >= lead * 10)
+    turn = jnp.where(idle, chunks, slots)
+    lax.fori_loop(0, turn, hop, 0)
 
     scores = nt(c_part, b_part)
     head_i = lax.broadcasted_iota(jnp.int32, (T, heads), 1)
@@ -298,6 +296,8 @@
     grad_inner = jnp.concatenate(pulls, axis=1)
     total = jnp.concatenate(mixes, axis=1)
 
+    lax.fori_loop(turn, slots, hop, 0)
+
     def settle(q, _):
         @pl.when(lon < lon_n - 1)
         def _():
@@ -336,8 +336,8 @@
     read_e = nt(c_part, ent_eb) * wide_ee
     read_w = nt(c_part, ent_wb) * wide_ew
     pull_e, pull_w = nt(b_part, adj_eb), nt(b_part, adj_wb)
-    mixed[...] = (total + read_e + read_w + gain[...] * inner).astype(BF16)
-    grad_inner = grad_inner + wide_fe * pull_e + wide_fw * pull_w + gain[...] * incoming
+    mixed[...] = (total + read_e + read_w + gain * inner).astype(BF16)
+    grad_inner = grad_inner + wide_fe * pull_e + wide_fw * pull_w + gain * incoming
     r_e, r_w = hi(read_e * incoming, gather), hi(read_w * incoming, gather)
     q_e, q_w = hi(pull_e * inner, gather), hi(pull_w * inner, gather)
     ones = jnp.ones((8, T), F32)
@@ -358,55 +358,134 @@
         (cols[2] / steps_r).T + far_e * q_e + far_w * q_w - rate_e * grad_log_e - rate_w * grad_log_w
     )
     grad_raw = grad_steps * jax.nn.sigmoid(shifted)
-    grad_step[...] = grad_raw
-    params[...] = jnp.zeros(params.shape, F32)
-    params[9:10, 0:heads] = jnp.sum(-steps * rate_e * grad_log_e, axis=0, keepdims=True)
-    params[10:11, 0:heads] = jnp.sum(-steps * rate_w * grad_log_w, axis=0, keepdims=True)
-    params[11:12, 0:heads] = jnp.sum(grad_raw, axis=0, keepdims=True)
-    params[12:13, 0:heads] = jnp.sum(hi(incoming * inner, gather), axis=0, keepdims=True)
-
-    def back(lanes, grad_active):
+    grad_step[...] = grad_raw.T
+    small = both // 128
+    params[small:8] = jnp.zeros((8 - small, 16, 128), F32)
+    params[0:small, 9:16] = jnp.zeros((small, 7, 128), F32)
+    params[small, 0:1, 0:heads] = jnp.sum(-steps * rate_e * grad_log_e, axis=0, keepdims=True)
+    params[small, 1:2, 0:heads] = jnp.sum(-steps * rate_w * grad_log_w, axis=0, keepdims=True)
+    params[small, 2:3, 0:heads] = jnp.sum(grad_raw, axis=0, keepdims=True)
+    params[small, 3:4, 0:heads] = jnp.sum(hi(incoming * inner, gather), axis=0, keepdims=True)
+
+    def back(part, grad_active):
+        lanes = slice(128 * part, 128 * part + 128)
         value = before[:, lanes]
         slope = jax.nn.sigmoid(value)
         grad = (
             grad_active.astype(BF16).astype(F32) * slope * (1.0 + value * (1.0 - slope))
         ).astype(BF16)
         grad_before[:, lanes] = grad
+
+    def weigh(part):
+        lanes = slice(128 * part, 128 * part + 128)
         edge = jnp.zeros((8, 128), F32)
-        wide = jnp.concatenate([edge, grad.astype(F32), edge], axis=0)
+        wide = jnp.concatenate([edge, grad_before[:, lanes].astype(F32), edge], axis=0)
         for b in range(3):
             moved = wide if b == 1 else pltpu.roll(wide, EXT - 1 if b == 0 else 1, 0)
             for a in range(3):
-                params[3 * a + b : 3 * a + b + 1, lanes] = jnp.sum(
+                params[part, 3 * a + b : 3 * a + b + 1] = jnp.sum(
                     moved * ext[a, :, lanes], axis=0, keepdims=True
                 )
 
-    for part in range(width // 128):
-        lanes = slice(128 * part, 128 * part + 128)
-        back(lanes, grad_inner[:, lanes])
+    parts_f = width // 128
+    for part in range(parts_f):
+        back(part, grad_inner[:, 128 * part : 128 * part + 128])
+    halo_f = halo_copies(grad_before.at[:, lanes_f], lanes_f, rows_g, edges_g, send_g, recv_g, 0)
+    for copy in halo_f:
+        copy.start()
+    for part in range(parts_f):
+        weigh(part)
     for copy in copies:
         copy.wait()
     proj = gathered[0]
     for d in range(1, tp_n):
         proj = proj + gathered[d]
     for part in range(2):
-        back(slice(width + 128 * part, width + 128 * part + 128), proj[:, 128 * part : 128 * part + 128])
+        back(parts_f + part, proj[:, 128 * part : 128 * part + 128])
+    halo_p = halo_copies(grad_before.at[:, lanes_p], lanes_p, rows_g, edges_g, send_g, recv_g, 8)
+    for copy in halo_p:
+        copy.start()
+    for part in range(2):
+        weigh(parts_f + part)
+
+    per_lat = 8 // lat_n
+    mine = pl.ds(lat * per_lat, per_lat)
+    share = [
+        pltpu.make_async_remote_copy(
+            params.at[pl.ds(other * per_lat, per_lat)], by_lat.at[lat], send_a.at[d], recv_a.at[d],
+            device_id={"lat": other}, device_id_type=MESH,
+        )
+        for d, other in enumerate(lat_others)
+    ]
+    for copy in share:
+        copy.start()
+    by_lat[pl.ds(lat, 1)] = params[mine][None]
+
+    def adjoint(part):
+        lanes = slice(128 * part, 128 * part + 128)
+        fill_extended(grad_before[:, lanes], lanes, rows_g, edges_g, ext_g)
+        value = stencil(ext_g, taps, lanes, True).astype(BF16)
+        if part < parts_f:
+            out_f[:, lanes] = value
+        else:
+            out_p[:, 128 * part - width : 128 * part - width + 128] = value
+
+    for copy in share:
+        copy.wait()
+    sums = by_lat[0]
+    for d in range(1, lat_n):
+        sums = sums + by_lat[d]
+    by_lon[pl.ds(lon, 1)] = sums[None]
+    share = [
+        pltpu.make_async_remote_copy(
+            by_lon.at[lon], by_lon.at[lon], send_b.at[d], recv_b.at[d],
+            device_id={"lon": other}, device_id_type=MESH,
+        )
+        for d, other in enumerate(lon_others)
+    ]
+    for copy in share:
+        copy.start()
+    for copy in halo_f + halo_p:
+        copy.wait()
+    for part in range(both // 128):
+        adjoint(part)
+    for copy in share:
+        copy.wait()
+    sums = by_lon[0]
+    for d in range(1, lon_n):
+        sums = sums + by_lon[d]
+    cells = T * lat_n * lon_n
+    whole[pl.ds(lat, 1)] = (sums * cells ** (-0.5))[None]
+    share = [
+        pltpu.make_async_remote_copy(
+            whole.at[lat], whole.at[lat], send_c.at[d], recv_c.at[d],
+            device_id={"lat": other}, device_id_type=MESH,
+        )
+        for d, other in enumerate(lat_others)
+    ]
+    for copy in share:
+        copy.start()
+    for copy in share:
+        copy.wait()
+    for part in range(both // 128):
+        tile = whole[part // per_lat, part % per_lat, 0:9, :]
+        if part < parts_f:
+            out_taps_f[:, 128 * part : 128 * part + 128] = tile
+        else:
+            out_taps_p[:, 128 * (part - parts_f) : 128 * (part - parts_f) + 128] = tile
+    tile = whole[small // per_lat, small % per_lat, 0:8, :]
+    out_logs[...] = tile[0:2, 0:heads]
+    out_bias[...] = tile[2:3, 0:heads]
+    out_gain[...] = tile[3:4, 0:heads]
+
+
+def finish_kernel(*refs):
+    count = len(refs) // 2
+    for source, target in zip(refs[:count], refs[count:]):
+        target[...] = source[...]
 
 
 VM = pl.BlockSpec(memory_space=pltpu.VMEM)
-
-
-def call(kernel, outs, scratch, ident, ins):
-    return pl.pallas_call(
-        kernel,
-        out_shape=outs,
-        in_specs=[VM] * len(ins),
-        out_specs=tuple(VM for _ in outs),
-        scratch_shapes=scratch,
-        compiler_params=pltpu.CompilerParams(
-            collective_id=ident, has_side_effects=True, vmem_limit_bytes=60 << 20
-        ),
-    )(*ins)
 
 
 def shards(
@@ -414,63 +493,59 @@
     conv_projections, state_east, state_west, cotangent,
 ):
     width, heads = features.shape[2], step_raw.shape[2]
-    both = width + projections.shape[2]
-    tp_n = lax.axis_size("tp")
+    extra = projections.shape[2]
+    both = width + extra
+    tp_n, lat_n, lon_n = lax.axis_size("tp"), lax.axis_size("lat"), lax.axis_size("lon")
     sds = jax.ShapeDtypeStruct
     dma = pltpu.SemaphoreType.DMA
-    joined = jnp.concatenate([features[0], projections[0]], axis=1)
-    taps = jnp.concatenate([conv_features, conv_projections], axis=1)
-    halo = [
-        pltpu.VMEM((2, T, both), BF16),
-        pltpu.VMEM((6, 16, both), BF16),
-        dma((8,)),
-        dma((8,)),
-    ]
-    ext_shape = (3, EXT, both)
-    before, active, ext = call(
-        conv_kernel,
-        (sds((T, both), F32), sds((T, both), BF16), sds(ext_shape, F32)),
-        halo,
-        0,
-        (joined, taps),
-    )
-    raw = step_raw[0]
+    vm = pltpu.VMEM
     flat = (width, T)
     chunks = 2 * heads
-    block = pltpu.VMEM((chunks, width // heads, T), F32)
-    mixed, grad_before, grad_step, params = call(
-        state_kernel,
-        (sds((T, width), BF16), sds((T, both), BF16), sds((T, heads), F32), sds((16, both), F32)),
-        [
+    block = vm((chunks, width // heads, T), F32)
+    outs = (
+        sds((T, width), BF16), sds((T, width), BF16), sds((T, extra), BF16), sds((heads, T), F32),
+        sds((9, width), F32), sds((9, extra), F32), sds((2, heads), F32), sds((1, heads), F32),
+        sds((1, heads), F32),
+    )
+    ins = (
+        features[0], projections[0], cotangent[0], step_raw[0].T, step_bias[None], decay_log,
+        skip_gain[None], conv_features, conv_projections, state_east.reshape(flat),
+        state_west.reshape(flat),
+    )
+    per_lat = 8 // lat_n
+    results = pl.pallas_call(
+        layer_kernel,
+        out_shape=outs,
+        in_specs=[VM] * len(ins),
+        out_specs=(VM,) * len(outs),
+        scratch_shapes=[
+            vm((T, both), F32), vm((T, both), BF16), vm((3, EXT, both), F32), vm((3, EXT, both), F32),
+            vm((T, both), BF16), vm((9, both), F32),
+            vm((2, T, both), BF16), vm((6, 16, both), BF16),
+            vm((2, T, both), BF16), vm((6, 16, both), BF16),
             block, block, block, block, block, block,
-            pltpu.VMEM((chunks, T), F32),
-            pltpu.VMEM((chunks, T), F32),
-            pltpu.VMEM((3, heads, T), F32),
-            pltpu.VMEM((tp_n, T, both - width), F32),
+            vm((chunks, T), F32), vm((chunks, T), F32), vm((3, heads, T), F32),
+            vm((tp_n, T, extra), F32),
+            vm((8, 16, 128), F32), vm((lat_n, per_lat, 16, 128), F32),
+            vm((lon_n, per_lat, 16, 128), F32), vm((lat_n, per_lat, 16, 128), F32),
+            dma((16,)), dma((16,)), dma((16,)), dma((16,)),
             dma((chunks,)), dma((chunks,)), dma((chunks,)), dma((chunks,)),
-            dma((tp_n - 1,)), dma((tp_n - 1,)),
+            dma((tp_n - 1,)), dma((tp_n - 1,)), dma((lat_n - 1,)), dma((lat_n - 1,)),
+            dma((lon_n - 1,)), dma((lon_n - 1,)), dma((lat_n - 1,)), dma((lat_n - 1,)),
         ],
-        1,
-        (
-            active, before, ext, cotangent[0], raw, raw.T, step_bias[None], step_bias[:, None],
-            decay_log, decay_log.T, jnp.repeat(skip_gain, width // heads)[None],
-            state_east.reshape(flat), state_west.reshape(flat),
+        compiler_params=pltpu.CompilerParams(
+            collective_id=0, has_side_effects=True, vmem_limit_bytes=60 << 20
         ),
-    )
-    totals = lax.psum(params, ("lon", "lat"))
-    grad_f, grad_p = call(
-        adjoint_kernel,
-        (sds((T, width), BF16), sds((T, both - width), BF16)),
-        [pltpu.VMEM(ext_shape, F32)] + halo,
-        2,
-        (grad_before, taps),
-    )
-    cells = T * lax.axis_size("lat") * lax.axis_size("lon")
-    totals = totals * cells ** (-0.5)
+    )(*ins)
+    mixed, grad_f, grad_p, grad_step, taps_f, taps_p, logs, bias, gain = pl.pallas_call(
+        finish_kernel,
+        out_shape=outs,
+        in_specs=[VM] * len(outs),
+        out_specs=(VM,) * len(outs),
+    )(*results)
     return (
-        mixed[None], grad_f[None], grad_p[None], grad_step[None],
-        totals[0:9, :width], totals[0:9, width:], totals[9:11, :heads],
-        totals[11, :heads], totals[12, :heads],
+        mixed[None], grad_f[None], grad_p[None], grad_step.T[None], taps_f, taps_p, logs,
+        bias[0], gain[0],
     )
 
 

time: 617 us -> 112 us (0.18)
  blocking collectives: 503 us -> 0 us
  Pallas kernels: 95 us -> 111 us
  local copies, waits for them, and re-layouts: 15.4 us -> 0 us
    psum x1 -> x0, blocking collectives: 503 us -> none  [shards(): totals = lax.psum(params, ('lon', 'lat'))]
    pallas_call x3 -> x2, Pallas kernels: 95 us -> 111 us  [the longest x1 109 us: shards(): pl.pallas_call(layer_kernel, out_shape=outs, in_specs=[VM] * len(ins), ou...]
    unnamed x8 -> x0, local copies, waits for them, and re-layouts: 8.22 us -> none
where the time goes in v2:
time: 112 us
  Pallas kernels  111 us (99%)
    pallas_call x1, Pallas kernels, shards(): pl.pallas_call(layer_kernel, out_shape=outs, in_specs=[VM] * len(ins), ou...  109 us

profile of v2, /device:TPU:1, one launch (start us, length us, event | category | flops | bytes accessed | tf_op | source)
XLA Modules:
  0.0 111.5 jit_solution(2020293259852382706)
XLA Ops:
  0.6 109.1 %shard_map.178 = (bf16[128,512]{1,0:T(8,128)(2,1)}, bf16[128,512]{1,0:T(8,128)(2,1)}, bf16[128,256]{1,0:T(8,128)(2,1)}, f32[8,128]{1,0:T(8,128)}, f32[9,512]{1,0...) custom-call(bf16[128,512]{1,0:T(8,128)(2,1)} %bitcast.20, ...), custom_call_target="tpu_custom_call" | custom-call | tf_op jit(solution)/shard_map/pallas_call | solution.py:516
  109.7 1.8 %shard_map.179 = (bf16[128,512]{1,0:T(8,128)(2,1)}, bf16[128,512]{1,0:T(8,128)(2,1)}, bf16[128,256]{1,0:T(8,128)(2,1)}, f32[8,128]{1,0:T(8,128)}, f32[9,512]{1,0...) custom-call(bf16[128,512]{1,0:T(8,128)(2,1)} %get-tuple-element.27.refs_0_, ...), custom_call_target="tpu_custom_call" | custom-call | tf_op jit(solution)/shard_map/pallas_call | solution.py:540

commit v3 on v2

--- a/solution.py
+++ b/solution.py
@@ -12,6 +12,7 @@
 BF16 = jnp.bfloat16
 T = 128
 EXT = T + 16
+CUT = 2
 EDGES = ((0, -1), (0, 1), (-1, -1), (-1, 1), (1, -1), (1, 1))
 
 
@@ -119,13 +120,12 @@
     width = cot.shape[1]
     both = width + projections.shape[1]
     size = width // heads
-    chunks = 2 * heads
+    split = CUT
+    chunks = 2 * heads * split
     tp_peers = [{"tp": lax.rem(tp + d, tp_n)} for d in range(1, tp_n)]
     lat_others = [lax.rem(lat + d, lat_n) for d in range(1, lat_n)]
     lon_others = [lax.rem(lon + d, lon_n) for d in range(1, lon_n)]
-    greet(
-        grid_peers() + tp_peers + [{"lat": o} for o in lat_others] + [{"lon": o} for o in lon_others]
-    )
+    greet(grid_peers() + tp_peers + [{"lat": o} for o in lat_others])
     lanes_f, lanes_p = pl.ds(0, width), pl.ds(width, both - width)
     halo = halo_copies(features, lanes_f, rows, edges, send_h, recv_h, 0)
     halo += halo_copies(projections, lanes_p, rows, edges, send_h, recv_h, 8)
@@ -162,12 +162,16 @@
     fac_e, fac_w = far_e * steps, far_w * steps
     wide_ee, wide_ew = hi(jnp.exp(sum_e), spread), hi(jnp.exp(sum_w), spread)
     wide_fe, wide_fw = hi(fac_e, spread), hi(fac_w, spread)
+    half = heads * split
     close_e = jnp.broadcast_to(jnp.exp(sum_er[:, T - 1 : T]), (heads, T))
     close_w = jnp.broadcast_to(jnp.exp(sum_wr[:, 0:1]), (heads, T))
-    dec_r[0:heads] = close_e
-    dec_r[heads:chunks] = close_w
-    dec_l[0:heads] = close_w
-    dec_l[heads:chunks] = close_e
+    for h in range(heads):
+        east = jnp.broadcast_to(close_e[h : h + 1], (split, T))
+        west = jnp.broadcast_to(close_w[h : h + 1], (split, T))
+        dec_r[h * split : (h + 1) * split] = east
+        dec_l[h * split : (h + 1) * split] = west
+        dec_r[half + h * split : half + (h + 1) * split] = west
+        dec_l[half + h * split : half + (h + 1) * split] = east
 
     gain = hi(jnp.broadcast_to(gain_r[...], (8, heads)), spread)[0:1]
 
@@ -190,21 +194,21 @@
     incoming = cot[...].astype(F32)
     src_e, src_w = (inner * wide_fe).astype(BF16), (inner * wide_fw).astype(BF16)
     inc_e, inc_w = (incoming * wide_ee).astype(BF16), (incoming * wide_ew).astype(BF16)
-    shape3 = (heads, size, T)
-    add_r[0:heads] = tn(src_e, b_part).reshape(shape3)
-    add_r[heads:chunks] = tn(inc_w, c_part).reshape(shape3)
-    add_l[0:heads] = tn(src_w, b_part).reshape(shape3)
-    add_l[heads:chunks] = tn(inc_e, c_part).reshape(shape3)
+    shape3 = (half, size // split, T)
+    add_r[0:half] = tn(src_e, b_part).reshape(shape3)
+    add_r[half:chunks] = tn(inc_w, c_part).reshape(shape3)
+    add_l[0:half] = tn(src_w, b_part).reshape(shape3)
+    add_l[half:chunks] = tn(inc_e, c_part).reshape(shape3)
 
     @pl.when(lon == 0)
     def _():
-        in_r[0:heads] = start_e[...].reshape(shape3)
-        in_r[heads:chunks] = jnp.zeros(shape3, F32)
+        in_r[0:half] = start_e[...].reshape(shape3)
+        in_r[half:chunks] = jnp.zeros(shape3, F32)
 
     @pl.when(lon == lon_n - 1)
     def _():
-        in_l[0:heads] = start_w[...].reshape(shape3)
-        in_l[heads:chunks] = jnp.zeros(shape3, F32)
+        in_l[0:half] = start_w[...].reshape(shape3)
+        in_l[half:chunks] = jnp.zeros(shape3, F32)
 
     def copy_r(q):
         return pltpu.make_async_remote_copy(
@@ -218,9 +222,10 @@
             device_id=grid_peer(0, -1), device_id_type=MESH,
         )
 
-    lead = 3
-    skew_r = jnp.maximum(0, (2 * lon - (lon_n - 1)) * lead)
-    skew_l = jnp.maximum(0, ((lon_n - 1) - 2 * lon) * lead)
+    lead = 6
+    ahead = 2 * lon - (lon_n - 1)
+    skew_r = jnp.clip(ahead * lead, 0, chunks)
+    skew_l = jnp.clip(-ahead * lead, 0, chunks)
 
     def hop(slot, _):
         q_r, q_l = slot - skew_r, slot - skew_l
@@ -249,8 +254,8 @@
 
         return 0
 
-    slots = chunks + lead * (lon_n - 1)
-    idle = (skew_r >= lead * 10) | (skew_l >= lead * 10)
+    slots = 2 * chunks
+    idle = jnp.abs(ahead) >= (2 * lon_n) // 3
     turn = jnp.where(idle, chunks, slots)
     lax.fori_loop(0, turn, hop, 0)
 
@@ -298,31 +303,31 @@
 
     lax.fori_loop(turn, slots, hop, 0)
 
-    def settle(q, _):
-        @pl.when(lon < lon_n - 1)
-        def _():
-            copy_r(q).wait_send()
-
-        @pl.when(lon > 0)
-        def _():
-            copy_l(q).wait_send()
-
-        return 0
-
-    lax.fori_loop(0, chunks, settle, 0)
-
     flat = (width, T)
-    ent_e, adj_w = in_r[0:heads].reshape(flat), in_r[heads:chunks].reshape(flat)
-    ent_w, adj_e = in_l[0:heads].reshape(flat), in_l[heads:chunks].reshape(flat)
+    ent_e, adj_w = in_r[0:half].reshape(flat), in_r[half:chunks].reshape(flat)
+    ent_w, adj_e = in_l[0:half].reshape(flat), in_l[half:chunks].reshape(flat)
     ent_eb, ent_wb = ent_e.astype(BF16), ent_w.astype(BF16)
     adj_eb, adj_wb = adj_e.astype(BF16), adj_w.astype(BF16)
 
     scores_b = grad_scores.astype(BF16)
     me = pl.ds(tp, 1)
-    grad_b = tn(scores_b, c_part) + nn(src_e, adj_eb) + nn(src_w, adj_wb)
-    grad_c = nn(scores_b, b_part) + nn(inc_e, ent_eb) + nn(inc_w, ent_wb)
-    gathered[me, :, 0:T] = grad_b[None]
-    gathered[me, :, T : 2 * T] = grad_c[None]
+    scores_t = (grad_scores - scores_b.astype(F32)).astype(BF16)
+
+    def low(value, rounded):
+        return (value - rounded.astype(F32)).astype(BF16)
+
+    grad_b = (
+        tn(scores_b, c_part) + tn(scores_t, c_part)
+        + nn(src_e, adj_eb) + nn(src_e, low(adj_e, adj_eb))
+        + nn(src_w, adj_wb) + nn(src_w, low(adj_w, adj_wb))
+    )
+    grad_c = (
+        nn(scores_b, b_part) + nn(scores_t, b_part)
+        + nn(inc_e, ent_eb) + nn(inc_e, low(ent_e, ent_eb))
+        + nn(inc_w, ent_wb) + nn(inc_w, low(ent_w, ent_wb))
+    )
+    gathered[me, :, 0:T] = grad_b.astype(BF16)[None]
+    gathered[me, :, T : 2 * T] = grad_c.astype(BF16)[None]
     copies = [
         pltpu.make_async_remote_copy(
             gathered.at[tp], gathered.at[tp], send_t.at[d], recv_t.at[d],
@@ -360,12 +365,11 @@
     grad_raw = grad_steps * jax.nn.sigmoid(shifted)
     grad_step[...] = grad_raw.T
     small = both // 128
-    params[small:8] = jnp.zeros((8 - small, 16, 128), F32)
-    params[0:small, 9:16] = jnp.zeros((small, 7, 128), F32)
-    params[small, 0:1, 0:heads] = jnp.sum(-steps * rate_e * grad_log_e, axis=0, keepdims=True)
-    params[small, 1:2, 0:heads] = jnp.sum(-steps * rate_w * grad_log_w, axis=0, keepdims=True)
-    params[small, 2:3, 0:heads] = jnp.sum(grad_raw, axis=0, keepdims=True)
-    params[small, 3:4, 0:heads] = jnp.sum(hi(incoming * inner, gather), axis=0, keepdims=True)
+    params[small:8] = jnp.zeros((8 - small, 8, 128), F32)
+    params[small + 1, 0:1, 0:heads] = jnp.sum(-steps * rate_e * grad_log_e, axis=0, keepdims=True)
+    params[small + 1, 1:2, 0:heads] = jnp.sum(-steps * rate_w * grad_log_w, axis=0, keepdims=True)
+    params[small + 1, 2:3, 0:heads] = jnp.sum(grad_raw, axis=0, keepdims=True)
+    params[small + 1, 3:4, 0:heads] = jnp.sum(hi(incoming * inner, gather), axis=0, keepdims=True)
 
     def back(part, grad_active):
         lanes = slice(128 * part, 128 * part + 128)
@@ -383,9 +387,11 @@
         for b in range(3):
             moved = wide if b == 1 else pltpu.roll(wide, EXT - 1 if b == 0 else 1, 0)
             for a in range(3):
-                params[part, 3 * a + b : 3 * a + b + 1] = jnp.sum(
-                    moved * ext[a, :, lanes], axis=0, keepdims=True
-                )
+                tap = jnp.sum(moved * ext[a, :, lanes], axis=0, keepdims=True)
+                if 3 * a + b < 8:
+                    params[part, 3 * a + b : 3 * a + b + 1] = tap
+                else:
+                    params[small, part : part + 1] = tap
 
     parts_f = width // 128
     for part in range(parts_f):
@@ -397,9 +403,9 @@
         weigh(part)
     for copy in copies:
         copy.wait()
-    proj = gathered[0]
+    proj = gathered[0].astype(F32)
     for d in range(1, tp_n):
-        proj = proj + gathered[d]
+        proj = proj + gathered[d].astype(F32)
     for part in range(2):
         back(parts_f + part, proj[:, 128 * part : 128 * part + 128])
     halo_p = halo_copies(grad_before.at[:, lanes_p], lanes_p, rows_g, edges_g, send_g, recv_g, 8)
@@ -465,15 +471,30 @@
     ]
     for copy in share:
         copy.start()
+
+    def settle(q, _):
+        @pl.when(lon < lon_n - 1)
+        def _():
+            copy_r(q).wait_send()
+
+        @pl.when(lon > 0)
+        def _():
+            copy_l(q).wait_send()
+
+        return 0
+
+    lax.fori_loop(0, chunks, settle, 0)
+
     for copy in share:
         copy.wait()
     for part in range(both // 128):
-        tile = whole[part // per_lat, part % per_lat, 0:9, :]
-        if part < parts_f:
-            out_taps_f[:, 128 * part : 128 * part + 128] = tile
-        else:
-            out_taps_p[:, 128 * (part - parts_f) : 128 * (part - parts_f) + 128] = tile
-    tile = whole[small // per_lat, small % per_lat, 0:8, :]
+        tile = whole[part // per_lat, part % per_lat]
+        last = whole[small // per_lat, small % per_lat, part : part + 1]
+        target = out_taps_f if part < parts_f else out_taps_p
+        lanes = slice(128 * (part % parts_f), 128 * (part % parts_f) + 128)
+        target[0:8, lanes] = tile
+        target[8:9, lanes] = last
+    tile = whole[(small + 1) // per_lat, (small + 1) % per_lat]
     out_logs[...] = tile[0:2, 0:heads]
     out_bias[...] = tile[2:3, 0:heads]
     out_gain[...] = tile[3:4, 0:heads]
@@ -500,8 +521,8 @@
     dma = pltpu.SemaphoreType.DMA
     vm = pltpu.VMEM
     flat = (width, T)
-    chunks = 2 * heads
-    block = vm((chunks, width // heads, T), F32)
+    chunks = 2 * heads * CUT
+    block = vm((chunks, width // heads // CUT, T), F32)
     outs = (
         sds((T, width), BF16), sds((T, width), BF16), sds((T, extra), BF16), sds((heads, T), F32),
         sds((9, width), F32), sds((9, extra), F32), sds((2, heads), F32), sds((1, heads), F32),
@@ -525,9 +546,9 @@
             vm((2, T, both), BF16), vm((6, 16, both), BF16),
             block, block, block, block, block, block,
             vm((chunks, T), F32), vm((chunks, T), F32), vm((3, heads, T), F32),
-            vm((tp_n, T, extra), F32),
-            vm((8, 16, 128), F32), vm((lat_n, per_lat, 16, 128), F32),
-            vm((lon_n, per_lat, 16, 128), F32), vm((lat_n, per_lat, 16, 128), F32),
+            vm((tp_n, T, extra), BF16),
+            vm((8, 8, 128), F32), vm((lat_n, per_lat, 8, 128), F32),
+            vm((lon_n, per_lat, 8, 128), F32), vm((lat_n, per_lat, 8, 128), F32),
             dma((16,)), dma((16,)), dma((16,)), dma((16,)),
             dma((chunks,)), dma((chunks,)), dma((chunks,)), dma((chunks,)),
             dma((tp_n - 1,)), dma((tp_n - 1,)), dma((lat_n - 1,)), dma((lat_n - 1,)),

time: 112 us -> 101 us (0.902)
  Pallas kernels: 111 us -> 101 us
    pallas_call x1, Pallas kernels: 109 us -> 98.9 us  [shards(): pl.pallas_call(layer_kernel, out_shape=outs, in_specs=[VM] * len(ins), ou...]
where the time goes in v3:
time: 101 us
  Pallas kernels  101 us (100%)
    pallas_call x1, Pallas kernels, shards(): pl.pallas_call(layer_kernel, out_shape=outs, in_specs=[VM] * len(ins), ou...  98.9 us

profile of v3, /device:TPU:1, one launch (start us, length us, event | category | flops | bytes accessed | tf_op | source)
XLA Modules:
  0.0 101.3 jit_solution(17882342888897933845)
XLA Ops:
  0.6 98.9 %shard_map.178 = (bf16[128,512]{1,0:T(8,128)(2,1)}, bf16[128,512]{1,0:T(8,128)(2,1)}, bf16[128,256]{1,0:T(8,128)(2,1)}, f32[8,128]{1,0:T(8,128)}, f32[9,512]{1,0...) custom-call(bf16[128,512]{1,0:T(8,128)(2,1)} %bitcast.20, ...), custom_call_target="tpu_custom_call" | custom-call | tf_op jit(solution)/shard_map/pallas_call | solution.py:537
  99.5 1.8 %shard_map.179 = (bf16[128,512]{1,0:T(8,128)(2,1)}, bf16[128,512]{1,0:T(8,128)(2,1)}, bf16[128,256]{1,0:T(8,128)(2,1)}, f32[8,128]{1,0:T(8,128)}, f32[9,512]{1,0...) custom-call(bf16[128,512]{1,0:T(8,128)(2,1)} %get-tuple-element.27.refs_0_, ...), custom_call_target="tpu_custom_call" | custom-call | tf_op jit(solution)/shard_map/pallas_call | solution.py:561

commit v4 on v3

--- a/solution.py
+++ b/solution.py
@@ -222,7 +222,7 @@
             device_id=grid_peer(0, -1), device_id_type=MESH,
         )
 
-    lead = 6
+    lead = 13
     ahead = 2 * lon - (lon_n - 1)
     skew_r = jnp.clip(ahead * lead, 0, chunks)
     skew_l = jnp.clip(-ahead * lead, 0, chunks)

time: 101 us -> 97.6 us (0.966)
  Pallas kernels: 101 us -> 96.8 us
    pallas_call x1, Pallas kernels: 98.9 us -> 95 us  [shards(): pl.pallas_call(layer_kernel, out_shape=outs, in_specs=[VM] * len(ins), ou...]
where the time goes in v4:
time: 97.6 us; the launch traced here: 97.5 us
  Pallas kernels  96.8 us (99%)
    pallas_call x1, Pallas kernels, shards(): pl.pallas_call(layer_kernel, out_shape=outs, in_specs=[VM] * len(ins), ou...  95 us

profile of v4, /device:TPU:1, one launch (start us, length us, event | category | flops | bytes accessed | tf_op | source)
XLA Modules:
  0.0 97.5 jit_solution(841205818596341054)
XLA Ops:
  0.6 95.0 %shard_map.178 = (bf16[128,512]{1,0:T(8,128)(2,1)}, bf16[128,512]{1,0:T(8,128)(2,1)}, bf16[128,256]{1,0:T(8,128)(2,1)}, f32[8,128]{1,0:T(8,128)}, f32[9,512]{1,0...) custom-call(bf16[128,512]{1,0:T(8,128)(2,1)} %bitcast.20, ...), custom_call_target="tpu_custom_call" | custom-call | tf_op jit(solution)/shard_map/pallas_call | solution.py:537
  95.7 1.8 %shard_map.179 = (bf16[128,512]{1,0:T(8,128)(2,1)}, bf16[128,512]{1,0:T(8,128)(2,1)}, bf16[128,256]{1,0:T(8,128)(2,1)}, f32[8,128]{1,0:T(8,128)}, f32[9,512]{1,0...) custom-call(bf16[128,512]{1,0:T(8,128)(2,1)} %get-tuple-element.27.refs_0_, ...), custom_call_target="tpu_custom_call" | custom-call | tf_op jit(solution)/shard_map/pallas_call | solution.py:561

commit v5 on v4

--- a/solution.py
+++ b/solution.py
@@ -45,6 +45,10 @@
     for peer in peers:
         pl.semaphore_signal(barrier, inc=1, device_id=peer, device_id_type=MESH)
     pl.semaphore_wait(barrier, len(peers))
+
+
+def far_first(count):
+    return sorted(range(1, count), key=lambda d: -min(d, count - d))
 
 
 def grid_peers():
@@ -122,9 +126,9 @@
     size = width // heads
     split = CUT
     chunks = 2 * heads * split
-    tp_peers = [{"tp": lax.rem(tp + d, tp_n)} for d in range(1, tp_n)]
-    lat_others = [lax.rem(lat + d, lat_n) for d in range(1, lat_n)]
-    lon_others = [lax.rem(lon + d, lon_n) for d in range(1, lon_n)]
+    tp_peers = [{"tp": lax.rem(tp + d, tp_n)} for d in far_first(tp_n)]
+    lat_others = [lax.rem(lat + d, lat_n) for d in far_first(lat_n)]
+    lon_others = [lax.rem(lon + d, lon_n) for d in far_first(lon_n)]
     greet(grid_peers() + tp_peers + [{"lat": o} for o in lat_others])
     lanes_f, lanes_p = pl.ds(0, width), pl.ds(width, both - width)
     halo = halo_copies(features, lanes_f, rows, edges, send_h, recv_h, 0)

time: 97.6 us -> 97.4 us (level)
  no operation moved by 1% of the time
where the time goes in v5:
time: 97.4 us; the launch traced here: 97.2 us
  Pallas kernels  96.6 us (99%)
    pallas_call x1, Pallas kernels, shards(): pl.pallas_call(layer_kernel, out_shape=outs, in_specs=[VM] * len(ins), ou...  94.7 us

profile of v5, /device:TPU:1, one launch (start us, length us, event | category | flops | bytes accessed | tf_op | source)
XLA Modules:
  0.0 97.2 jit_solution(12330390907583524166)
XLA Ops:
  0.6 94.7 %shard_map.178 = (bf16[128,512]{1,0:T(8,128)(2,1)}, bf16[128,512]{1,0:T(8,128)(2,1)}, bf16[128,256]{1,0:T(8,128)(2,1)}, f32[8,128]{1,0:T(8,128)}, f32[9,512]{1,0...) custom-call(bf16[128,512]{1,0:T(8,128)(2,1)} %bitcast.20, ...), custom_call_target="tpu_custom_call" | custom-call | tf_op jit(solution)/shard_map/pallas_call | solution.py:541
  95.4 1.8 %shard_map.179 = (bf16[128,512]{1,0:T(8,128)(2,1)}, bf16[128,512]{1,0:T(8,128)(2,1)}, bf16[128,256]{1,0:T(8,128)(2,1)}, f32[8,128]{1,0:T(8,128)}, f32[9,512]{1,0...) custom-call(bf16[128,512]{1,0:T(8,128)(2,1)} %get-tuple-element.27.refs_0_, ...), custom_call_target="tpu_custom_call" | custom-call | tf_op jit(solution)/shard_map/pallas_call | solution.py:565
